TPU v7x, 256 devices: a whole 4x4x8 slice. The times are simulated.
256 devices in a mesh: slab: 4 (over y), freq: 64 (over z, x, core).
Axes of the slice: x: 4, y: 4, z: 8, core: 2. Of those that a mesh axis runs over, the one named last changes fastest.
Arguments:
- initial: float32 [2, 512, 128, 256], P(None, 'freq', 'slab'), may hold values from -6 to 6
- measured: float32 [2, 512, 128, 256], P(None, 'freq', 'slab'), may hold values from -6 to 6
- projector: bfloat16 [3, 2, 512, 256, 256], P(None, None, 'freq'), may hold values from -0.15625 to 0.15625
- offsets: int32 [3], replicated, may hold values from -16 to 16, as said below
Outputs:
- volume: float32 [128, 256, 1024], P('slab', 'freq')
Inputs may be any that keep to these rules, and one draw needn't show every extreme that they name: `offsets`: the first entry is +16 or -16; the third is its negative; the second lies strictly between -16 and 16.
All inputs are finite; a program needn't handle non-finite values.
Results may differ from a plain program's by a relative error of at most 0.005.
Values may be sent and summed in bfloat16 or wider, within the bound.
No kernel may reach another device: no remote copies, remote signals or barrier semaphores. Data moves between devices by JAX's collectives and lax.ppermute only.
A program may use at most 128 MiB of HBM per device.

v0:
```python
import math

import jax
import jax.numpy as jnp
import numpy as np
from jax import lax
from jax.experimental import pallas as pl
from jax.experimental.pallas import tpu as pltpu
from jax.sharding import PartitionSpec as P

A = 1024
Q = A // 4
STEP_SIZE = 0.25
CLIP_LEVEL = 1.0
SMOOTHING = 0.25
INNER = 2
SLABS = 4
GROUPS = 64
Z = 128
R = 256
F32 = jnp.float32
BF16 = jnp.bfloat16
SEND_INPUT = jnp.float16
SEND_OUT = (BF16, F32)
SEND_BACK = BF16
VMEM = pl.BlockSpec(memory_space=pltpu.VMEM)
SMEM = pl.BlockSpec(memory_space=pltpu.SMEM)
ANY = pl.BlockSpec(memory_space=pl.ANY)


def split_table(table):
    high = table.astype(np.float32).astype(jnp.bfloat16)
    low = (table - high.astype(np.float64)).astype(np.float32).astype(jnp.bfloat16)
    return high, low


def tables():
    group, half, part = np.meshgrid(np.arange(GROUPS), np.arange(2), np.arange(2), indexing="ij")
    plain, turned, weights = [], [], []
    for residue in range(4):
        k = (8 * group + residue + 4 * half).reshape(-1)
        imag = part.reshape(-1)[:, None] == 1
        phase = (k[:, None] * np.arange(Q)[None, :] % A) * (2.0 * math.pi / A)
        plain.append(np.where(imag, -np.sin(phase), np.cos(phase)) / math.sqrt(A))
        turned.append(np.where(imag, -np.cos(phase), -np.sin(phase)) / math.sqrt(A))
        weights.append(np.where(k == 0, 1.0, 2.0)[:, None])
    synth = [(p * w).T for p, w in zip(plain, weights)]
    synth_turned = [(t * w).T for t, w in zip(turned, weights)]
    to_angles = np.concatenate(
        [synth[0], synth[2], synth[1], synth_turned[1], synth[3], synth_turned[3]], axis=0
    )
    even = np.concatenate([plain[0], plain[2]], axis=0)
    odd = np.concatenate(
        [np.concatenate([plain[c], turned[c]], axis=1) for c in (1, 3)], axis=0
    )
    return split_table(to_angles), split_table(even), split_table(odd)


def dot(left, right):
    return jnp.dot(left, right, preferred_element_type=F32)


def prepare_kernel(slab_ref, projector_ref, plain_ref, turned_ref, sems):
    slab = slab_ref[0]
    copies = []
    for half in range(2):
        for part in range(2):
            for slot in range(3):
                copy = pltpu.make_async_copy(
                    projector_ref.at[slot, part, slab + 4 * half],
                    plain_ref.at[half, part, :, pl.ds(R * slot, R)],
                    sems.at[len(copies)],
                )
                copy.start()
                copies.append(copy)
    index = 0
    for half in range(2):
        for part in range(2):
            for slot in range(3):
                copies[index].wait()
                index += 1
                cols = pl.ds(R * slot, R)
                turned_ref[half, part, :, cols] = plain_ref[half, part, :, cols].T


def prepare(slab, projector):
    shape = jax.ShapeDtypeStruct((2, 2, R, 3 * R), BF16)
    return pl.pallas_call(
        prepare_kernel,
        out_shape=(shape, shape),
        in_specs=[SMEM, ANY],
        out_specs=(VMEM, VMEM),
        scratch_shapes=[pltpu.SemaphoreType.DMA((12,))],
        cost_estimate=pl.CostEstimate(flops=0, bytes_accessed=8 << 20, transcendentals=0),
        name="prepare",
    )(slab, projector)


def moved(values, offset, lane):
    source = lane + offset
    rolled = pltpu.roll(values, lax.rem(Z - offset, Z), 1)
    return jnp.where((source >= 0) & (source < Z), rolled, 0.0).astype(BF16)


def swap_blocks(blocks):
    lane = lax.broadcasted_iota(jnp.int32, blocks[0].shape, 1)
    odd32 = (lane // 32) % 2 == 1
    high64 = lane >= 64
    a, b, c, d = blocks
    for_pairs = []
    for low, high in ((a, b), (c, d)):
        for_pairs.append(
            (
                jnp.where(odd32, pltpu.roll(high, 32, 1), low),
                jnp.where(odd32, high, pltpu.roll(low, 96, 1)),
            )
        )
    (a, b), (c, d) = for_pairs
    out = [None] * 4
    for i, (low, high) in enumerate(((a, c), (b, d))):
        out[i] = jnp.where(high64, pltpu.roll(high, 64, 1), low)
        out[i + 2] = jnp.where(high64, high, pltpu.roll(low, 64, 1))
    return out


def passes(offsets_ref, plain_ref, turned_ref, iterate, measured, shifted):
    lane = lax.broadcasted_iota(jnp.int32, (R, Z), 1)

    def step(count, carry):
        half = lax.rem(count, 2)
        for slot in range(3):
            rows = pl.ds(R * slot, R)
            offset = offsets_ref[slot]
            shifted[rows, :Z] = moved(iterate[half, 0], offset, lane)
            shifted[rows, Z:] = moved(iterate[half, 1], offset, lane)
        by_real = dot(turned_ref[half, 0], shifted[...])
        by_imag = dot(turned_ref[half, 1], shifted[...])
        real = measured[half, 0] - (by_real[:, :Z] - by_imag[:, Z:])
        imag = measured[half, 1] - (by_imag[:, :Z] + by_real[:, Z:])
        real = real.astype(BF16).astype(F32)
        imag = imag.astype(BF16).astype(F32)
        for slot in range(3):
            rows = pl.ds(R * slot, R)
            offset = -offsets_ref[slot]
            shifted[rows, :Z] = moved(real, offset, lane)
            shifted[rows, Z:] = moved(imag, offset, lane)
        by_real = dot(plain_ref[half, 0], shifted[...])
        by_imag = dot(plain_ref[half, 1], shifted[...])
        iterate[half, 0] += STEP_SIZE * (by_real[:, :Z] + by_imag[:, Z:])
        iterate[half, 1] += STEP_SIZE * (by_real[:, Z:] - by_imag[:, :Z])
        return carry

    lax.fori_loop(0, 2 * INNER, step, 0)


def pack(iterate, rows_ref, packed_ref):
    for half in range(2):
        for part in range(2):
            blocks = [iterate[half, part, pl.ds(i, GROUPS, stride=4), :] for i in range(4)]
            for slab, block in enumerate(swap_blocks(blocks)):
                rows_ref[pl.ds(Q * slab + 2 * half + part, GROUPS, stride=4), :] = block
    packed_ref[...] = rows_ref[...].astype(packed_ref.dtype)


def first_kernel(
    slab_ref, offsets_ref, own, one, two, three, plain_ref, turned_ref,
    packed_ref, measured_out, column, iterate, shifted, rows_ref,
):
    slab = slab_ref[0]
    for array, target in ((0, iterate), (1, measured_out)):
        for half in range(2):
            for part in range(2):
                for distance, piece in enumerate((own, one, two, three)):
                    start = 32 * lax.rem(slab + 4 - distance, 4)
                    column[pl.ds(pl.multiple_of(start, 32), 32), :] = piece[array, part, half].astype(F32)
                target[half, part] = column[...].T
    passes(offsets_ref, plain_ref, turned_ref, iterate, measured_out, shifted)
    pack(iterate, rows_ref, packed_ref)


def second_kernel(
    offsets_ref, packed_in, measured_ref, plain_ref, turned_ref,
    packed_ref, iterate, shifted, rows_ref,
):
    rows_ref[...] = packed_in[...].astype(F32)
    for half in range(2):
        for part in range(2):
            blocks = [
                rows_ref[pl.ds(Q * slab + 2 * half + part, GROUPS, stride=4), :] for slab in range(4)
            ]
            for i, block in enumerate(swap_blocks(blocks)):
                iterate[half, part, pl.ds(i, GROUPS, stride=4), :] = block
    passes(offsets_ref, plain_ref, turned_ref, iterate, measured_ref, shifted)
    pack(iterate, rows_ref, packed_ref)


def pass_scratch():
    return [
        pltpu.VMEM((2, 2, R, Z), F32),
        pltpu.VMEM((3 * R, 2 * Z), BF16),
        pltpu.VMEM((4 * Q, Z), F32),
    ]


PASS_COST = pl.CostEstimate(flops=2 << 30, bytes_accessed=8 << 20, transcendentals=0)


def first_half(slab, offsets, pieces, plain, turned, send_type):
    return pl.pallas_call(
        first_kernel,
        out_shape=(
            jax.ShapeDtypeStruct((4 * Q, Z), send_type),
            jax.ShapeDtypeStruct((2, 2, R, Z), F32),
        ),
        in_specs=[SMEM, SMEM] + [VMEM] * 6,
        out_specs=(VMEM, VMEM),
        scratch_shapes=[pltpu.VMEM((Z, R), F32)] + pass_scratch(),
        cost_estimate=PASS_COST,
        name="first_half",
    )(slab, offsets, *pieces, plain, turned)


def later_half(offsets, packed, measured, plain, turned, send_type):
    return pl.pallas_call(
        second_kernel,
        out_shape=jax.ShapeDtypeStruct((4 * Q, Z), send_type),
        in_specs=[SMEM] + [VMEM] * 4,
        out_specs=VMEM,
        scratch_shapes=pass_scratch(),
        cost_estimate=PASS_COST,
        name="later_half",
    )(offsets, packed, measured, plain, turned)


def to_volume(packed_ref, high_ref, low_ref, volume):
    def residue(c, rows):
        block = packed_ref[pl.ds(Q * c, Q), :]
        if block.dtype == BF16:
            return dot(high_ref[rows, :], block) + dot(low_ref[rows, :], block)
        high = block.astype(BF16)
        low = (block - high.astype(F32)).astype(BF16)
        both = dot(high_ref[rows, :], jnp.concatenate([high, low], axis=1))
        return both[:, :Z] + both[:, Z:] + dot(low_ref[rows, :], high)

    zero = residue(0, pl.ds(0, Q))
    two = residue(2, pl.ds(Q, Q))
    same, other = zero + two, zero - two
    one = residue(1, pl.ds(2 * Q, 2 * Q))
    three = residue(3, pl.ds(4 * Q, 2 * Q))
    plain = one[:Q] + three[:Q]
    turned = one[Q:] - three[Q:]
    volume[pl.ds(8, Q), :] = same + plain
    volume[pl.ds(8 + Q, Q), :] = other + turned
    volume[pl.ds(8 + 2 * Q, Q), :] = same - plain
    volume[pl.ds(8 + 3 * Q, Q), :] = other - turned
    volume[7:8, :] = volume[A + 7 : A + 8, :]
    volume[A + 8 : A + 9, :] = volume[8:9, :]


def smooth(volume, start):
    here = volume[pl.ds(8 + start, Q), :]
    before = volume[pl.ds(7 + start, Q), :]
    after = volume[pl.ds(9 + start, Q), :]
    ahead = jnp.clip(after - here, -CLIP_LEVEL, CLIP_LEVEL)
    behind = jnp.clip(here - before, -CLIP_LEVEL, CLIP_LEVEL)
    return here - SMOOTHING * (behind - ahead)


def split(values):
    high = values.astype(BF16)
    return high, (values - high.astype(F32)).astype(BF16)


def wide_dot(high_table, low_table, values):
    high, low = split(values)
    both = dot(high_table, jnp.concatenate([high, low], axis=1))
    return both[:, :Z] + both[:, Z:] + dot(low_table, high)


def middle_kernel(
    packed_ref, high_ref, low_ref, even_high, even_low, odd_high, odd_low, spectra_ref, volume
):
    to_volume(packed_ref, high_ref, low_ref, volume)
    quarters = [smooth(volume, Q * m) for m in range(4)]
    same, cross = quarters[0] + quarters[2], quarters[1] + quarters[3]
    plain, turned = quarters[0] - quarters[2], quarters[1] - quarters[3]

    def put(c, values):
        spectra_ref[pl.ds(Q * c, Q), :] = values.astype(spectra_ref.dtype)

    put(0, wide_dot(even_high[:Q], even_low[:Q], same + cross))
    put(2, wide_dot(even_high[Q:], even_low[Q:], same - cross))
    put(1, wide_dot(odd_high[:Q], odd_low[:Q], jnp.concatenate([plain, turned], axis=0)))
    put(3, wide_dot(odd_high[Q:], odd_low[Q:], jnp.concatenate([plain, -turned], axis=0)))


def middle(packed, angles, even, odd):
    return pl.pallas_call(
        middle_kernel,
        out_shape=jax.ShapeDtypeStruct((4 * Q, Z), SEND_BACK),
        in_specs=[VMEM] * 7,
        out_specs=VMEM,
        scratch_shapes=[pltpu.VMEM((A + 16, Z), F32)],
        cost_estimate=pl.CostEstimate(flops=1 << 30, bytes_accessed=4 << 20, transcendentals=0),
        name="middle",
    )(packed, *angles, *even, *odd)


def last_kernel(packed_ref, high_ref, low_ref, out_ref, volume):
    to_volume(packed_ref, high_ref, low_ref, volume)
    for m in range(4):
        values = smooth(volume, Q * m).T
        for i in range(4):
            out_ref[:, i, pl.ds(Q * m, Q)] = values[32 * i : 32 * (i + 1), :]


def last(packed, angles):
    return pl.pallas_call(
        last_kernel,
        out_shape=jax.ShapeDtypeStruct((Z // SLABS, R // GROUPS, A), F32),
        in_specs=[VMEM] * 3,
        out_specs=VMEM,
        scratch_shapes=[pltpu.VMEM((A + 16, Z), F32)],
        cost_estimate=pl.CostEstimate(flops=1 << 29, bytes_accessed=4 << 20, transcendentals=0),
        name="last",
    )(packed, *angles)


def exchange(packed):
    blocks = packed.reshape(SLABS * GROUPS, 4, Z)
    return lax.all_to_all(blocks, ("slab", "freq"), 0, 0, tiled=True).reshape(packed.shape)


def on_device(initial, measured, projector, offsets):
    angles, even, odd = tables()
    slab = lax.axis_index("slab").astype(jnp.int32)
    both = jnp.stack([initial, measured]).astype(SEND_INPUT)
    both = both.reshape(2, 2, 2, SLABS, *initial.shape[2:])
    pieces = []
    for distance in range(SLABS):
        piece = lax.dynamic_index_in_dim(both, lax.rem(slab + distance, SLABS), 3, keepdims=False)
        if distance:
            piece = lax.ppermute(piece, "slab", [(i, (i + distance) % SLABS) for i in range(SLABS)])
        pieces.append(piece.astype(F32))
    slab = slab.reshape(1)
    plain, turned = prepare(slab, projector)
    packed, measured = first_half(slab, offsets, pieces, plain, turned, SEND_OUT[0])
    packed = exchange(middle(exchange(packed), angles, even, odd))
    packed = later_half(offsets, packed, measured, plain, turned, SEND_OUT[1])
    return last(exchange(packed), angles)


def solution(mesh):
    placed = (
        P(None, "freq", "slab", None),
        P(None, "freq", "slab", None),
        P(None, None, "freq", None, None),
        P(),
    )
    return jax.shard_map(
        on_device, mesh=mesh, in_specs=placed, out_specs=P("slab", "freq", None), check_vma=False
    )
```

profile of v0, /device:TPU:1, one launch (start us, length us, event | category | flops | bytes accessed | tf_op | source)
XLA Modules:
  0.0 116.7 jit_solution(14994692646352279333)
XLA Ops:
  0.0 1.1 convert.9
  1.1 1.1 convert.10
  2.2 0.8 fusion.1
  3.0 3.6 %collective-permute-start.2 = (f16[2,2,2,32,256]{4,3,2,1,0:T(8,128)(2,1)S(1)}, f16[2,2,2,32,256]{4,3,2,1,0:T(8,128)(2,1)S(1)}, u32[]{:S(2)}, u32[]{:S(2)}) collective-permute-start(f16[2,2,2,32,256]{4,3,2,1,0:T(8,128)(2,1)S(1)} %get-tuple-element.13), channel_id=1, source_target_pairs={{0,192},{64,0},{128,64},{192,128},{1,193},{65,1},{129,65},{193,129... | collective-permute-start | bytes 393224 | tf_op jit(solution)/shard_map/ppermute | solution.py:343
  6.6 0.0 collective-permute-start
  6.6 1.6 %collective-permute-start.1 = (f16[2,2,2,32,256]{4,3,2,1,0:T(8,128)(2,1)S(1)}, f16[2,2,2,32,256]{4,3,2,1,0:T(8,128)(2,1)S(1)}, u32[]{:S(2)}, u32[]{:S(2)}) collective-permute-start(f16[2,2,2,32,256]{4,3,2,1,0:T(8,128)(2,1)S(1)} %get-tuple-element.16), channel_id=1, source_target_pairs={{0,128},{64,192},{128,0},{192,64},{1,129},{65,193},{129,1},{193,65... | collective-permute-start | bytes 393224 | tf_op jit(solution)/shard_map/ppermute | solution.py:343
  8.2 3.6 %prepare.1 = (bf16[2,2,256,768]{3,2,1,0:T(8,128)(2,1)}, bf16[2,2,256,768]{3,2,1,0:T(8,128)(2,1)}) custom-call(s32[1]{0:T(128)} %bitcast.slab_ref, bf16[3,2,8,256,256]{4,3,2,1,0:T(8,128)(2,1)} %projector_ref.1), custom_call_target="tpu_custom_call" | custom-call | bytes 8388608 | tf_op jit(solution)/shard_map/prepare/pallas_call | solution.py:88
  11.9 0.0 collective-permute-done.2
  11.9 0.7 convert_element_type.20.three
  12.6 2.6 %collective-permute-done = f16[2,2,2,32,256]{4,3,2,1,0:T(8,128)(2,1)S(1)} collective-permute-done((f16[2,2,2,32,256]{4,3,2,1,0:T(8,128)(2,1)S(1)}, f16[2,2,2,32,256]{4,3,2,1,0:T(8,128)(2,1)S(1)}, u32[]{:S(2)}, u32[]{:S(2)}) %collective-permute-start) | collective-permute-done | bytes 131104 | tf_op jit(solution)/shard_map/ppermute | solution.py:343
  15.2 0.7 convert_element_type.18.one
  15.9 0.0 collective-permute-done.1
  15.9 0.7 convert_element_type.19.two
  16.7 7.8 %first_half.1 = (bf16[1024,128]{1,0:T(8,128)(2,1)}, f32[2,2,256,128]{3,2,1,0:T(8,128)}) custom-call(s32[1]{0:T(128)} %bitcast.slab_ref, s32[3]{0:T(128)} %offsets_ref.3, f32[2,2,2,32,256]{4,3,2,1,0:T(8,128)} %get-tuple-element.14.own, f32[2,2,2,32,256]{4,3,2,1,0:T(8,128)} %convert_element_type.18.one, f32[2,2,2,32,256]{4,3,2,1,0:T(8,128)} %convert_element_type.19.two, ...), custom_call_target="tpu_custom_call" | custom-call | flops 2147483648 | bytes 8388608 | tf_op jit(solution)/shard_map/first_half/pallas_call | solution.py:209
  24.4 28.4 %all_to_all.15 = bf16[256,4,128]{2,1,0:T(4,128)(2,1)} all-to-all(bf16[256,4,128]{2,1,0:T(4,128)(2,1)} %bitcast.32), channel_id=1, replica_groups=mesh['slab'=4,'freq'=64] {'slab','freq'}, dimensions={0} | all-to-all | bytes 524288 | tf_op jit(solution)/shard_map/all_to_all | solution.py:331
  52.8 4.3 %middle.1 = bf16[1024,128]{1,0:T(8,128)(2,1)} custom-call(bf16[1024,128]{1,0:T(8,128)(2,1)} %bitcast.33, bf16[1536,256]{1,0:T(8,128)(2,1)} %constant.45.clone.high_ref, bf16[1536,256]{1,0:T(8,128)(2,1)} %constant.46.clone.low_ref, bf16[512,256]{1,0:T(8,128)(2,1)} %constant.47.clone.even_high, bf16[512,256]{1,0:T(8,128)(2,1)} %constant.48.clone.even_low, ...), custom_call_target="tpu_custom_call" | custom-call | flops 1073741824 | bytes 4194304 | tf_op jit(solution)/shard_map/middle/pallas_call | solution.py:298
  57.2 21.8 %all_to_all.16 = bf16[256,4,128]{2,1,0:T(4,128)(2,1)} all-to-all(bf16[256,4,128]{2,1,0:T(4,128)(2,1)} %bitcast.34), channel_id=1, replica_groups=mesh['slab'=4,'freq'=64] {'slab','freq'}, dimensions={0} | all-to-all | bytes 524288 | tf_op jit(solution)/shard_map/all_to_all | solution.py:331
  79.0 7.7 %later_half.1 = f32[1024,128]{1,0:T(8,128)} custom-call(s32[3]{0:T(128)} %offsets_ref.3, bf16[1024,128]{1,0:T(8,128)(2,1)} %bitcast.35, f32[2,2,256,128]{3,2,1,0:T(8,128)} %get-tuple-element.12.measured_ref, bf16[2,2,256,768]{3,2,1,0:T(8,128)(2,1)} %get-tuple-element.9.plain_ref, bf16[2,2,256,768]{3,2,1,0:T(8,128)(2,1)} %get-tuple-element.10.turned_ref), custom_call_target="tpu_custom_call" | custom-call | flops 2147483648 | bytes 8388608 | tf_op jit(solution)/shard_map/later_half/pallas_call | solution.py:224
  86.6 26.9 %all_to_all.17 = f32[256,4,128]{2,1,0:T(4,128)} all-to-all(f32[256,4,128]{2,1,0:T(4,128)} %bitcast.31), channel_id=1, replica_groups=mesh['slab'=4,'freq'=64] {'slab','freq'}, dimensions={0} | all-to-all | bytes 1048576 | tf_op jit(solution)/shard_map/all_to_all | solution.py:331
  113.5 3.2 %last.1 = f32[32,4,1024]{2,1,0:T(4,128)} custom-call(f32[1024,128]{1,0:T(8,128)} %bitcast.28, bf16[1536,256]{1,0:T(8,128)(2,1)} %constant.45.clone.high_ref, bf16[1536,256]{1,0:T(8,128)(2,1)} %constant.46.clone.low_ref), custom_call_target="tpu_custom_call" | custom-call | flops 536870912 | bytes 4194304 | tf_op jit(solution)/shard_map/last/pallas_call | solution.py:318
Async XLA Ops:
  3.0 8.9 %collective-permute-start.2 = (f16[2,2,2,32,256]{4,3,2,1,0:T(8,128)(2,1)S(1)}, f16[2,2,2,32,256]{4,3,2,1,0:T(8,128)(2,1)S(1)}, u32[]{:S(2)}, u32[]{:S(2)}) collective-permute-start(f16[2,2,2,32,256]{4,3,2,1,0:T(8,128)(2,1)S(1)} %get-tuple-element.13), channel_id=1, source_target_pairs={{0,192},{64,0},{128,64},{192,128},{1,193},{65,1},{129,65},{193,129... | collective-permute-start | bytes 393224 | tf_op jit(solution)/shard_map/ppermute | solution.py:343
  6.6 8.6 %collective-permute-start = (f16[2,2,2,32,256]{4,3,2,1,0:T(8,128)(2,1)S(1)}, f16[2,2,2,32,256]{4,3,2,1,0:T(8,128)(2,1)S(1)}, u32[]{:S(2)}, u32[]{:S(2)}) collective-permute-start(f16[2,2,2,32,256]{4,3,2,1,0:T(8,128)(2,1)S(1)} %get-tuple-element.15), channel_id=1, source_target_pairs={{0,64},{64,128},{128,192},{192,0},{1,65},{65,129},{129,193},{193,1... | collective-permute-start | bytes 393224 | tf_op jit(solution)/shard_map/ppermute | solution.py:343
  6.6 9.4 %collective-permute-start.1 = (f16[2,2,2,32,256]{4,3,2,1,0:T(8,128)(2,1)S(1)}, f16[2,2,2,32,256]{4,3,2,1,0:T(8,128)(2,1)S(1)}, u32[]{:S(2)}, u32[]{:S(2)}) collective-permute-start(f16[2,2,2,32,256]{4,3,2,1,0:T(8,128)(2,1)S(1)} %get-tuple-element.16), channel_id=1, source_target_pairs={{0,128},{64,192},{128,0},{192,64},{1,129},{65,193},{129,1},{193,65... | collective-permute-start | bytes 393224 | tf_op jit(solution)/shard_map/ppermute | solution.py:343
where the time goes:
time: 117 us
  blocking collectives  77.1 us (66%)
  Pallas kernels  26.6 us (23%)
  starting transfers between devices  5.2 us (4%)
  other arithmetic  5.14 us (4%)
  waiting for transfers between devices  2.61 us (2%)
    all_to_all x3, blocking collectives, exchange(): lax.all_to_all(blocks, ('slab', 'freq'), 0, 0, tiled=True)  77.1 us
    pallas_call x1, Pallas kernels, first_half(): pl.pallas_call(first_kernel, out_shape=(jax.ShapeDtypeStruct((4 * Q, Z),...  7.76 us
    pallas_call x1, Pallas kernels, later_half(): pl.pallas_call(second_kernel, out_shape=jax.ShapeDtypeStruct((4 * Q, Z),...  7.7 us
    ppermute x3, starting transfers between devices, on_device(): lax.ppermute(piece, 'slab', [(i, (i + distance) % SLABS) for i in range(S...  5.2 us
    pallas_call x1, Pallas kernels, middle(): pl.pallas_call(middle_kernel, out_shape=jax.ShapeDtypeStruct((4 * Q, Z),...  4.32 us
    pallas_call x1, Pallas kernels, prepare(): pl.pallas_call(prepare_kernel, out_shape=(shape, shape), in_specs=[SMEM,...  3.65 us
    pallas_call x1, Pallas kernels, last(): pl.pallas_call(last_kernel, out_shape=jax.ShapeDtypeStruct((Z // SLABS, R...  3.21 us
    ppermute x3, waiting for transfers between devices, on_device(): lax.ppermute(piece, 'slab', [(i, (i + distance) % SLABS) for i in range(S...  2.61 us
  transfers between devices with their start and end apart: 3, of which 1 were waited for; matrix products, arithmetic and copies ran while one was open for 1% of the time, Pallas kernels for 3%

commit v1 on v0

v1 whole, which is shorter than its diff:
```python
import math

import jax
import jax.numpy as jnp
import numpy as np
from jax import lax
from jax.experimental import pallas as pl
from jax.experimental.pallas import tpu as pltpu
from jax.sharding import PartitionSpec as P

A = 1024
Q = A // 4
STEP_SIZE = 0.25
CLIP_LEVEL = 1.0
SMOOTHING = 0.25
INNER = 2
SLABS = 4
GROUPS = 64
Z = 128
R = 256
F32 = jnp.float32
BF16 = jnp.bfloat16
LEVELS = 32000.0
VMEM = pl.BlockSpec(memory_space=pltpu.VMEM)
SMEM = pl.BlockSpec(memory_space=pltpu.SMEM)
HBM = pl.BlockSpec(memory_space=pltpu.HBM)


def split_table(table):
    high = table.astype(np.float32).astype(jnp.bfloat16)
    low = (table - high.astype(np.float64)).astype(np.float32).astype(jnp.bfloat16)
    return high, low


def tables():
    group, half, part = np.meshgrid(np.arange(GROUPS), np.arange(2), np.arange(2), indexing="ij")
    plain, turned, weights = [], [], []
    for residue in range(4):
        k = (8 * group + residue + 4 * half).reshape(-1)
        imag = part.reshape(-1)[:, None] == 1
        phase = (k[:, None] * np.arange(Q)[None, :] % A) * (2.0 * math.pi / A)
        plain.append(np.where(imag, -np.sin(phase), np.cos(phase)) / math.sqrt(A))
        turned.append(np.where(imag, -np.cos(phase), -np.sin(phase)) / math.sqrt(A))
        weights.append(np.where(k == 0, 1.0, 2.0)[:, None])
    synth = [(p * w).T for p, w in zip(plain, weights)]
    synth_turned = [(t * w).T for t, w in zip(turned, weights)]
    to_angles = np.concatenate(
        [synth[0], synth[2], synth[1], synth_turned[1], synth[3], synth_turned[3]], axis=0
    )
    even = np.concatenate([plain[0], plain[2]], axis=0)
    odd = np.concatenate(
        [np.concatenate([plain[c], turned[c]], axis=1) for c in (1, 3)], axis=0
    )
    return split_table(to_angles), split_table(even), split_table(odd)


def cost(flops, size):
    return pl.CostEstimate(flops=flops, bytes_accessed=size, transcendentals=0)


PARAMS = pltpu.CompilerParams(vmem_limit_bytes=20 << 20)
ALONE = pltpu.CompilerParams(vmem_limit_bytes=100 << 19)
SPECTRUM = jax.ShapeDtypeStruct((2, R, Z), F32)
PACKED = jax.ShapeDtypeStruct((4 * Q, Z), BF16)


def dot(left, right):
    return jnp.dot(left, right, preferred_element_type=F32)


def prepare_kernel(slab_ref, projector_ref, blocks_ref, blocks, sems):
    slab = slab_ref[0]
    loads, stores = [], []
    for half in range(2):
        for part in range(2):
            for slot in range(3):
                copy = pltpu.make_async_copy(
                    projector_ref.at[slot, part, slab + 4 * half],
                    blocks.at[half, 2 + part, :, pl.ds(R * slot, R)],
                    sems.at[len(loads)],
                )
                copy.start()
                loads.append(copy)
    for half in range(2):
        for part in range(2):
            for slot in range(3):
                loads[6 * half + 3 * part + slot].wait()
                cols = pl.ds(R * slot, R)
                blocks[half, part, :, cols] = blocks[half, 2 + part, :, cols].T
        copy = pltpu.make_async_copy(blocks.at[half], blocks_ref.at[half], sems.at[12 + half])
        copy.start()
        stores.append(copy)
    for copy in stores:
        copy.wait()


def prepare(slab, projector):
    return pl.pallas_call(
        prepare_kernel,
        out_shape=jax.ShapeDtypeStruct((4, 4, R, 3 * R), BF16),
        in_specs=[SMEM, HBM],
        out_specs=HBM,
        scratch_shapes=[pltpu.VMEM((2, 4, R, 3 * R), BF16), pltpu.SemaphoreType.DMA((14,))],
        compiler_params=ALONE,
        cost_estimate=cost(0, 8 << 20),
        name="prepare",
    )(slab, projector)


def encode(values):
    largest = jnp.max(jnp.max(jnp.abs(values), axis=1, keepdims=True), axis=0, keepdims=True)
    power = jnp.clip(jnp.ceil(jnp.log2(largest)), -100.0, 100.0)
    return jnp.round(values * (LEVELS * jnp.exp2(-power))).astype(jnp.int32), power


def arrange_kernel(slab_ref, initial_ref, measured_ref, own_ref, *piece_refs):
    slab = slab_ref[0]
    row = lax.broadcasted_iota(jnp.int32, (16, Z), 0)
    for array, source in enumerate((initial_ref, measured_ref)):
        for part in range(2):
            own_ref[array, part] = source[part, slab]
    for distance, piece_ref in enumerate(piece_refs, 1):
        index = lax.rem(slab + distance, SLABS)
        head = jnp.zeros((16, Z), jnp.int32)
        for array, source in enumerate((initial_ref, measured_ref)):
            for part in range(2):
                block = 2 * array + part
                codes, power = encode(source[part, index])
                codes = codes.astype(jnp.int16)
                piece_ref[pl.ds(64 * block, 32), :] = codes[:, :Z]
                piece_ref[pl.ds(64 * block + 32, 32), :] = codes[:, Z:]
                head = jnp.where(row == block, power.astype(jnp.int32), head)
        piece_ref[pl.ds(256, 16), :] = head.astype(jnp.int16)


def arrange(slab, initial, measured, half):
    block = pl.BlockSpec((2, SLABS, 32, R), lambda i: (0, half, 0, 0))
    piece = jax.ShapeDtypeStruct((272, Z), jnp.int16)
    return pl.pallas_call(
        arrange_kernel,
        grid=(1,),
        out_shape=(jax.ShapeDtypeStruct((2, 2, 32, R), F32),) + (piece,) * 3,
        in_specs=[SMEM, block, block],
        out_specs=(VMEM,) * 4,
        compiler_params=pltpu.CompilerParams(vmem_limit_bytes=123 << 19),
        cost_estimate=cost(1 << 20, 1 << 20),
        name="arrange",
    )(slab, initial, measured)


def moved(values, offset, lane):
    source = lane + offset
    rolled = pltpu.roll(values, lax.rem(Z - offset, Z), 1)
    return jnp.where((source >= 0) & (source < Z), rolled, 0.0).astype(BF16)


def swap_blocks(blocks):
    lane = lax.broadcasted_iota(jnp.int32, blocks[0].shape, 1)
    odd32 = (lane // 32) % 2 == 1
    high64 = lane >= 64
    a, b, c, d = blocks
    for_pairs = []
    for low, high in ((a, b), (c, d)):
        for_pairs.append(
            (
                jnp.where(odd32, pltpu.roll(high, 32, 1), low),
                jnp.where(odd32, high, pltpu.roll(low, 96, 1)),
            )
        )
    (a, b), (c, d) = for_pairs
    out = [None] * 4
    for i, (low, high) in enumerate(((a, c), (b, d))):
        out[i] = jnp.where(high64, pltpu.roll(high, 64, 1), low)
        out[i + 2] = jnp.where(high64, high, pltpu.roll(low, 64, 1))
    return out


def passes(offsets_ref, projectors, iterates, measures, shifted):
    lane = lax.broadcasted_iota(jnp.int32, (R, Z), 1)

    def place(slot_sign, index, real, imag):
        for slot in range(3):
            rows = pl.ds(R * slot, R)
            offset = slot_sign * offsets_ref[slot]
            shifted[index, rows, :Z] = moved(real, offset, lane)
            shifted[index, rows, Z:] = moved(imag, offset, lane)

    def step(count, carry):
        for index, blocks in enumerate(projectors):
            iterate, measured = iterates[index], measures[index]
            place(1, index, iterate[0], iterate[1])
            by_real = dot(blocks[0], shifted[index])
            by_imag = dot(blocks[1], shifted[index])
            real = measured[0] - (by_real[:, :Z] - by_imag[:, Z:])
            imag = measured[1] - (by_imag[:, :Z] + by_real[:, Z:])
            place(-1, index, real.astype(BF16).astype(F32), imag.astype(BF16).astype(F32))
            by_real = dot(blocks[2], shifted[index])
            by_imag = dot(blocks[3], shifted[index])
            iterate[0] += STEP_SIZE * (by_real[:, :Z] + by_imag[:, Z:])
            iterate[1] += STEP_SIZE * (by_real[:, Z:] - by_imag[:, :Z])
        return carry

    lax.fori_loop(0, INNER, step, 0)


def pack(iterates, rows_ref, packed_ref):
    for half, iterate in enumerate(iterates):
        for part in range(2):
            blocks = [iterate[part, pl.ds(i, GROUPS, stride=4), :] for i in range(4)]
            for slab, block in enumerate(swap_blocks(blocks)):
                rows_ref[pl.ds(Q * slab + 2 * half + part, GROUPS, stride=4), :] = block
    packed_ref[...] = rows_ref[...].astype(packed_ref.dtype)


def load_blocks(blocks_far, blocks, sems, halves):
    copies = []
    for index, half in enumerate(halves):
        for kind in range(2):
            pair = pl.ds(2 * kind, 2)
            copy = pltpu.make_async_copy(
                blocks_far.at[half, pair], blocks.at[index, pair], sems.at[len(copies)]
            )
            copy.start()
            copies.append(copy)
    return copies


def gather(slab_ref, own, pieces, column, iterate, measured):
    slab = slab_ref[0]
    scales = [
        jnp.exp2(piece[pl.ds(256, 16), :].astype(jnp.int32).astype(F32)) * (1.0 / LEVELS)
        for piece in pieces
    ]
    for array, target in ((0, iterate), (1, measured)):
        for part in range(2):
            block = 2 * array + part
            column[pl.ds(pl.multiple_of(32 * slab, 32), 32), :] = own[array, part]
            for distance, (piece, scale) in enumerate(zip(pieces, scales), 1):
                rows = pl.ds(pl.multiple_of(32 * lax.rem(slab + 4 - distance, 4), 32), 32)
                for side in range(2):
                    codes = piece[pl.ds(64 * block + 32 * side, 32), :].astype(jnp.int32)
                    column[rows, Z * side : Z * (side + 1)] = codes.astype(F32) * scale[block : block + 1]
            target[part] = column[...].T


def early_kernel(
    slab_ref, offsets_ref, own, one, two, three, blocks_far,
    iterate, measured, column, shifted, blocks, sems,
):
    copies = load_blocks(blocks_far, blocks, sems, (0,))
    gather(slab_ref, own, (one, two, three), column, iterate, measured)
    for copy in copies:
        copy.wait()
    passes(offsets_ref, [blocks.at[0]], [iterate], [measured], shifted)


def late_kernel(
    slab_ref, offsets_ref, own, one, two, three, blocks_far, other,
    iterate, measured, packed_ref, column, shifted, blocks, sems, rows_ref,
):
    copies = load_blocks(blocks_far, blocks, sems, (1,))
    gather(slab_ref, own, (one, two, three), column, iterate, measured)
    for copy in copies:
        copy.wait()
    passes(offsets_ref, [blocks.at[0]], [iterate], [measured], shifted)
    pack([other, iterate], rows_ref, packed_ref)


def second_kernel(
    silent_ref, offsets_ref, packed_in, kept_0, kept_1, measured_0, measured_1, blocks_far,
    packed_ref, iterate, shifted, rows_ref, blocks, sems,
):
    copies = load_blocks(blocks_far, blocks, sems, (0, 1))
    rows_ref[...] = packed_in[...].astype(F32)
    silent = silent_ref[0] != 0
    for half, kept in enumerate((kept_0, kept_1)):
        for part in range(2):
            parts = [
                rows_ref[pl.ds(Q * slab + 2 * half + part, GROUPS, stride=4), :] for slab in range(4)
            ]
            for i, added in enumerate(swap_blocks(parts)):
                rows = pl.ds(i, GROUPS, stride=4)
                base = kept[part, rows, :]
                if half == 0 and part == 1:
                    base = jnp.where(silent, 0.0, base)
                iterate[half, part, rows, :] = base + added
    for copy in copies:
        copy.wait()
    iterates = [iterate.at[0], iterate.at[1]]
    passes(offsets_ref, [blocks.at[0], blocks.at[1]], iterates, [measured_0, measured_1], shifted)
    pack(iterates, rows_ref, packed_ref)


def pass_scratch(halves, sems):
    return [
        pltpu.VMEM((halves, 3 * R, 2 * Z), BF16),
        pltpu.VMEM((halves, 4, R, 3 * R), BF16),
        pltpu.SemaphoreType.DMA((sems,)),
    ]


ROWS = pltpu.VMEM((4 * Q, Z), F32)


def first_half(slab, offsets, pieces, blocks, other):
    late = other is not None
    return pl.pallas_call(
        late_kernel if late else early_kernel,
        out_shape=(SPECTRUM, SPECTRUM) + ((PACKED,) if late else ()),
        in_specs=[SMEM, SMEM] + [VMEM] * 4 + [HBM] + ([VMEM] if late else []),
        out_specs=(VMEM,) * (3 if late else 2),
        scratch_shapes=[pltpu.VMEM((Z, R), F32)] + pass_scratch(1, 2) + ([ROWS] if late else []),
        compiler_params=ALONE,
        cost_estimate=cost(1 << 30, 4 << 20),
        name="late" if late else "early",
    )(slab, offsets, *pieces, blocks, *((other,) if late else ()))


def later_half(silent, offsets, packed, kept, measures, blocks):
    shifted, held, sems = pass_scratch(2, 4)
    return pl.pallas_call(
        second_kernel,
        out_shape=PACKED,
        in_specs=[SMEM, SMEM] + [VMEM] * 5 + [HBM],
        out_specs=VMEM,
        scratch_shapes=[pltpu.VMEM((2, 2, R, Z), F32), shifted, ROWS, held, sems],
        compiler_params=ALONE,
        cost_estimate=cost(2 << 30, 8 << 20),
        name="later_half",
    )(silent, offsets, packed, *kept, *measures, blocks)


def to_volume(packed_ref, tables_ref, volume):
    def residue(c, rows):
        block = packed_ref[pl.ds(Q * c, Q), :]
        total = dot(tables_ref[0][rows, :], block)
        for table in tables_ref[1:]:
            total = total + dot(table[rows, :], block)
        return total

    zero = residue(0, pl.ds(0, Q))
    two = residue(2, pl.ds(Q, Q))
    same, other = zero + two, zero - two
    one = residue(1, pl.ds(2 * Q, 2 * Q))
    three = residue(3, pl.ds(4 * Q, 2 * Q))
    plain = one[:Q] + three[:Q]
    turned = one[Q:] - three[Q:]
    volume[pl.ds(8, Q), :] = same + plain
    volume[pl.ds(8 + Q, Q), :] = other + turned
    volume[pl.ds(8 + 2 * Q, Q), :] = same - plain
    volume[pl.ds(8 + 3 * Q, Q), :] = other - turned
    volume[7:8, :] = volume[A + 7 : A + 8, :]
    volume[A + 8 : A + 9, :] = volume[8:9, :]


def change(volume, start):
    here = volume[pl.ds(8 + start, Q), :]
    before = volume[pl.ds(7 + start, Q), :]
    after = volume[pl.ds(9 + start, Q), :]
    ahead = jnp.clip(after - here, -CLIP_LEVEL, CLIP_LEVEL)
    behind = jnp.clip(here - before, -CLIP_LEVEL, CLIP_LEVEL)
    return here, SMOOTHING * (ahead - behind)


def middle_kernel(packed_ref, angles_ref, even_ref, odd_ref, spectra_ref, volume):
    to_volume(packed_ref, [angles_ref], volume)
    quarters = [change(volume, Q * m)[1] for m in range(4)]
    same, cross = quarters[0] + quarters[2], quarters[1] + quarters[3]
    plain, turned = quarters[0] - quarters[2], quarters[1] - quarters[3]

    def put(c, table, *values):
        values = jnp.concatenate([v.astype(BF16) for v in values], axis=0)
        spectra_ref[pl.ds(Q * c, Q), :] = dot(table, values).astype(spectra_ref.dtype)

    put(0, even_ref[:Q], same + cross)
    put(2, even_ref[Q:], same - cross)
    put(1, odd_ref[:Q], plain, turned)
    put(3, odd_ref[Q:], plain, -turned)


def middle(packed, angles, even, odd):
    return pl.pallas_call(
        middle_kernel,
        out_shape=PACKED,
        in_specs=[VMEM] * 4,
        out_specs=VMEM,
        scratch_shapes=[pltpu.VMEM((A + 16, Z), F32)],
        compiler_params=PARAMS,
        cost_estimate=cost(1 << 30, 4 << 20),
        name="middle",
    )(packed, angles, even, odd)


def last_kernel(packed_ref, high_ref, low_ref, out_ref, volume):
    to_volume(packed_ref, [high_ref, low_ref], volume)
    for m in range(4):
        here, added = change(volume, Q * m)
        values = (here + added).T
        for i in range(4):
            out_ref[:, i, pl.ds(Q * m, Q)] = values[32 * i : 32 * (i + 1), :]


def last(packed, high, low):
    return pl.pallas_call(
        last_kernel,
        out_shape=jax.ShapeDtypeStruct((Z // SLABS, R // GROUPS, A), F32),
        in_specs=[VMEM] * 3,
        out_specs=VMEM,
        scratch_shapes=[pltpu.VMEM((A + 16, Z), F32)],
        compiler_params=PARAMS,
        cost_estimate=cost(1 << 29, 4 << 20),
        name="last",
    )(packed, high, low)


def exchange(packed):
    blocks = packed.reshape(SLABS * GROUPS, 4, Z)
    return lax.all_to_all(blocks, ("slab", "freq"), 0, 0, tiled=True).reshape(packed.shape)


def spread(slab, initial, measured, half):
    own, *pieces = arrange(slab, initial, measured, half)
    for distance, piece in enumerate(pieces, 1):
        pairs = [(i, (i + distance) % SLABS) for i in range(SLABS)]
        pieces[distance - 1] = lax.ppermute(piece, "slab", pairs)
    return [own, *pieces]


def on_device(initial, measured, projector, offsets):
    (angles, angles_low), (even, _), (odd, _) = tables()
    slab = lax.axis_index("slab").astype(jnp.int32)
    group = lax.axis_index("freq").astype(jnp.int32)
    silent = ((slab == 0) & (group == 0)).astype(jnp.int32).reshape(1)
    slab = slab.reshape(1)
    pieces = [spread(slab, initial, measured, half) for half in range(2)]
    blocks = prepare(slab, projector)
    kept_0, measured_0 = first_half(slab, offsets, pieces[0], blocks, None)
    late, kept_0 = lax.optimization_barrier((pieces[1], kept_0))
    kept_1, measured_1, packed = first_half(slab, offsets, late, blocks, kept_0)
    packed = exchange(middle(exchange(packed), angles, even, odd))
    packed = later_half(silent, offsets, packed, (kept_0, kept_1), (measured_0, measured_1), blocks)
    return last(exchange(packed), angles, angles_low)


def solution(mesh):
    placed = (
        P(None, "freq", "slab", None),
        P(None, "freq", "slab", None),
        P(None, None, "freq", None, None),
        P(),
    )
    return jax.shard_map(
        on_device, mesh=mesh, in_specs=placed, out_specs=P("slab", "freq", None), check_vma=False
    )
```

time: 117 us -> 106 us (0.906)
  blocking collectives: 77.1 us -> 51.4 us
  waiting for transfers between devices: 2.61 us -> 15.3 us
  starting transfers between devices: 5.2 us -> 14.1 us
  other arithmetic: 5.14 us -> 0 us
  Pallas kernels: 26.6 us -> 24.9 us
    all_to_all x3 -> x2, blocking collectives: 77.1 us -> 51.4 us  [exchange(): lax.all_to_all(blocks, ('slab', 'freq'), 0, 0, tiled=True)]
    all_to_all x0 -> x1, waiting for transfers between devices: none -> 15.3 us  [exchange(): lax.all_to_all(blocks, ('slab', 'freq'), 0, 0, tiled=True)]
    all_to_all x0 -> x1, starting transfers between devices: none -> 5.35 us  [exchange(): lax.all_to_all(blocks, ('slab', 'freq'), 0, 0, tiled=True)]
    ppermute x3 -> x6, starting transfers between devices: 5.2 us -> 8.77 us  [spread(): pieces[distance - 1] = lax.ppermute(piece, 'slab', pairs)]
    ppermute x3 -> x6, waiting for transfers between devices: 2.61 us -> 0.02 us  [spread(): pieces[distance - 1] = lax.ppermute(piece, 'slab', pairs)]
    another operation x2 -> x0, other arithmetic: 2.16 us -> none
    convert_element_type x3 -> x0, other arithmetic: 2.15 us -> none  [on_device(): pieces.append(piece.astype(F32))]
    pallas_call x1, Pallas kernels: 3.21 us -> 1.69 us  [last(): pl.pallas_call(last_kernel, out_shape=jax.ShapeDtypeStruct((Z // SLABS, R...]
  transfers between devices with their start and end apart: 3 -> 7, of which waited for: 1 -> 1; matrix products, arithmetic and copies ran while one was open for 1% -> 0% of each run, Pallas kernels for 3% -> 8%
where the time goes in v1:
time: 106 us
  blocking collectives  51.4 us (48%)
  Pallas kernels  24.9 us (23%)
  waiting for transfers between devices  15.3 us (14%)
  starting transfers between devices  14.1 us (13%)
    all_to_all x2, blocking collectives, exchange(): lax.all_to_all(blocks, ('slab', 'freq'), 0, 0, tiled=True)  51.4 us
    all_to_all x1, waiting for transfers between devices, exchange(): lax.all_to_all(blocks, ('slab', 'freq'), 0, 0, tiled=True)  15.3 us
    ppermute x6, starting transfers between devices, spread(): pieces[distance - 1] = lax.ppermute(piece, 'slab', pairs)  8.77 us
    pallas_call x2, Pallas kernels, first_half(): pl.pallas_call(late_kernel if late else early_kernel, out_shape=(SPECTRUM...  8.27 us
    pallas_call x1, Pallas kernels, later_half(): pl.pallas_call(second_kernel, out_shape=PACKED, in_specs=[SMEM, SMEM] + [...  6.19 us
    all_to_all x1, starting transfers between devices, exchange(): lax.all_to_all(blocks, ('slab', 'freq'), 0, 0, tiled=True)  5.35 us
    pallas_call x2, Pallas kernels, arrange(): pl.pallas_call(arrange_kernel, grid=(1,), out_shape=(jax.ShapeDtypeStruct...  3.76 us
    pallas_call x1, Pallas kernels, prepare(): pl.pallas_call(prepare_kernel, out_shape=jax.ShapeDtypeStruct((4, 4, R, 3...  3.22 us
  transfers between devices with their start and end apart: 7, of which 1 were waited for; matrix products, arithmetic and copies ran while one was open for 0% of the time, Pallas kernels for 8%

profile of v1, /device:TPU:1, one launch (start us, length us, event | category | flops | bytes accessed | tf_op | source)
XLA Modules:
  0.0 105.9 jit_solution(16623592008825335169)
XLA Ops:
  0.0 1.9 %arrange.3 = (f32[2,2,32,256]{3,2,1,0:T(8,128)}, s16[272,128]{1,0:T(8,128)(2,1)}, s16[272,128]{1,0:T(8,128)(2,1)}, s16[272,128]{1,0:T(8,128)(2,1)}) custom-call(s32[1]{0:T(128)} %bitcast.1.slab_ref, f32[2,8,32,256]{3,2,1,0:T(8,128)} %initial_ref.3, f32[2,8,32,256]{3,2,1,0:T(8,128)} %measured_ref.3), custom_call_target="tpu_custom_call" | custom-call | flops 1048576 | bytes 1048576 | tf_op jit(solution)/shard_map/arrange/pallas_call | solution.py:139
  1.9 2.1 %collective-permute-start.3 = (s16[272,128]{1,0:T(8,128)(2,1)}, s16[272,128]{1,0:T(8,128)(2,1)S(1)}, u32[]{:S(2)}, u32[]{:S(2)}) collective-permute-start(s16[272,128]{1,0:T(8,128)(2,1)} %get-tuple-element.28), channel_id=1, source_target_pairs={{0,64},{64,128},{128,192},{192,0},{1,65},{65,129},{129,193},{193,1... | collective-permute-start | bytes 208904 | tf_op jit(solution)/shard_map/ppermute | solution.py:425
  4.0 2.6 %collective-permute-start.4 = (s16[272,128]{1,0:T(8,128)(2,1)}, s16[272,128]{1,0:T(8,128)(2,1)S(1)}, u32[]{:S(2)}, u32[]{:S(2)}) collective-permute-start(s16[272,128]{1,0:T(8,128)(2,1)} %get-tuple-element.29), channel_id=1, source_target_pairs={{0,128},{64,192},{128,0},{192,64},{1,129},{65,193},{129,1},{193,65... | collective-permute-start | bytes 208904 | tf_op jit(solution)/shard_map/ppermute | solution.py:425
  6.6 1.1 %collective-permute-start.5 = (s16[272,128]{1,0:T(8,128)(2,1)}, s16[272,128]{1,0:T(8,128)(2,1)S(1)}, u32[]{:S(2)}, u32[]{:S(2)}) collective-permute-start(s16[272,128]{1,0:T(8,128)(2,1)} %get-tuple-element.30), channel_id=1, source_target_pairs={{0,192},{64,0},{128,64},{192,128},{1,193},{65,1},{129,65},{193,129... | collective-permute-start | bytes 208904 | tf_op jit(solution)/shard_map/ppermute | solution.py:425
  7.7 1.9 %arrange.2 = (f32[2,2,32,256]{3,2,1,0:T(8,128)}, s16[272,128]{1,0:T(8,128)(2,1)}, s16[272,128]{1,0:T(8,128)(2,1)}, s16[272,128]{1,0:T(8,128)(2,1)}) custom-call(s32[1]{0:T(128)} %bitcast.1.slab_ref, f32[2,8,32,256]{3,2,1,0:T(8,128)} %initial_ref.3, f32[2,8,32,256]{3,2,1,0:T(8,128)} %measured_ref.3), custom_call_target="tpu_custom_call" | custom-call | flops 1048576 | bytes 1048576 | tf_op jit(solution)/shard_map/arrange/pallas_call | solution.py:139
  9.6 0.4 collective-permute-start
  10.0 0.8 collective-permute-start.1
  10.8 3.2 %prepare.1.blocks_far = bf16[4,4,256,768]{3,2,1,0:T(8,128)(2,1)} custom-call(s32[1]{0:T(128)} %bitcast.1.slab_ref, bf16[3,2,8,256,256]{4,3,2,1,0:T(8,128)(2,1)} %projector_ref.1), custom_call_target="tpu_custom_call" | custom-call | bytes 8388608 | tf_op jit(solution)/shard_map/prepare/pallas_call | solution.py:98
  14.0 0.0 copy-start.2
  14.0 0.0 collective-permute-done.3.one
  14.0 1.8 %collective-permute-start.2 = (s16[272,128]{1,0:T(8,128)(2,1)S(1)}, s16[272,128]{1,0:T(8,128)(2,1)S(1)}, u32[]{:S(2)}, u32[]{:S(2)}) collective-permute-start(s16[272,128]{1,0:T(8,128)(2,1)S(1)} %copy-done.7), channel_id=1, source_target_pairs={{0,192},{64,0},{128,64},{192,128},{1,193},{65,1},{129,65},{193,129... | collective-permute-start | bytes 208904 | tf_op jit(solution)/shard_map/ppermute | solution.py:425
  15.8 0.0 copy-start
  15.8 0.0 copy-start.5
  15.9 0.0 copy-start.6
  15.9 3.9 %early.1 = (f32[2,256,128]{2,1,0:T(8,128)S(1)}, f32[2,256,128]{2,1,0:T(8,128)S(1)}) custom-call(s32[1]{0:T(128)} %bitcast.1.slab_ref, s32[3]{0:T(128)S(1)} %copy-done.4, f32[2,2,32,256]{3,2,1,0:T(8,128)S(1)} %copy-done.3, s16[272,128]{1,0:T(8,128)(2,1)S(1)} %collective-permute-done.3.one, s16[272,128]{1,0:T(8,128)(2,1)S(1)} %collective-permute-done.4.two, ...), custom_call_target="tpu_custom_call" | custom-call | flops 1073741824 | bytes 4194304 | tf_op jit(solution)/shard_map/early/pallas_call | solution.py:307
  19.8 4.4 %late.1 = (f32[2,256,128]{2,1,0:T(8,128)S(1)}, f32[2,256,128]{2,1,0:T(8,128)S(1)}, bf16[1024,128]{1,0:T(8,128)(2,1)S(1)}) custom-call(s32[1]{0:T(128)} %bitcast.1.slab_ref, s32[3]{0:T(128)S(1)} %copy-done.4, f32[2,2,32,256]{3,2,1,0:T(8,128)S(1)} %copy-done.2, s16[272,128]{1,0:T(8,128)(2,1)S(1)} %collective-permute-done.one, ...), custom_call_target="tpu_custom_call" | custom-call | flops 1073741824 | bytes 4194304 | tf_op jit(solution)/shard_map/late/pallas_call | solution.py:307
  24.2 31.0 %all_to_all.15 = bf16[256,4,128]{2,1,0:T(4,128)(2,1)S(1)} all-to-all(bf16[256,4,128]{2,1,0:T(4,128)(2,1)S(1)} %bitcast.10), channel_id=1, replica_groups=mesh['slab'=4,'freq'=64] {'slab','freq'}, dimensions={0} | all-to-all | bytes 524288 | tf_op jit(solution)/shard_map/all_to_all | solution.py:418
  55.2 0.0 copy-start.1
  55.2 1.7 %middle.1 = bf16[1024,128]{1,0:T(8,128)(2,1)} custom-call(bf16[1024,128]{1,0:T(8,128)(2,1)S(1)} %bitcast.12, bf16[1536,256]{1,0:T(8,128)(2,1)S(1)} %copy-done, bf16[512,256]{1,0:T(8,128)(2,1)S(1)} %copy-done.6, bf16[512,512]{1,0:T(8,128)(2,1)S(1)} %copy-done.5), custom_call_target="tpu_custom_call" | custom-call | flops 1073741824 | bytes 4194304 | tf_op jit(solution)/shard_map/middle/pallas_call | solution.py:382
  56.9 5.3 %all-to-all-start.1 = ((bf16[256,4,128]{2,1,0:T(4,128)(2,1)}), bf16[256,4,128]{2,1,0:T(4,128)(2,1)S(1)}, u32[]{:S(2)}, u32[]{:S(2)}) async-start(bf16[256,4,128]{2,1,0:T(4,128)(2,1)} %bitcast.4), calls=%async_computation.1 | async-start | bytes 524288 | tf_op jit(solution)/shard_map/all_to_all | solution.py:418
  62.3 15.3 %all-to-all-done.1 = bf16[256,4,128]{2,1,0:T(4,128)(2,1)S(1)} async-done(((bf16[256,4,128]{2,1,0:T(4,128)(2,1)}), bf16[256,4,128]{2,1,0:T(4,128)(2,1)S(1)}, u32[]{:S(2)}, u32[]{:S(2)}) %all-to-all-start.1) | async-done | bytes 262176 | tf_op jit(solution)/shard_map/all_to_all | solution.py:418
  77.6 6.2 %later_half.1 = bf16[1024,128]{1,0:T(8,128)(2,1)S(1)} custom-call(s32[1]{0:T(128)} %bitcast.silent_ref, s32[3]{0:T(128)S(1)} %copy-done.4, bf16[1024,128]{1,0:T(8,128)(2,1)S(1)} %bitcast.9, f32[2,256,128]{2,1,0:T(8,128)S(1)} %get-tuple-element.36.other.kept_0, f32[2,256,128]{2,1,0:T(8,128)S(1)} %get-tuple-element.38.kept_1, ...), custom_call_target="tpu_custom_call" | custom-call | flops 2147483648 | bytes 8388608 | tf_op jit(solution)/shard_map/later_half/pallas_call | solution.py:321
  83.8 20.4 %all_to_all.16 = bf16[256,4,128]{2,1,0:T(4,128)(2,1)S(1)} all-to-all(bf16[256,4,128]{2,1,0:T(4,128)(2,1)S(1)} %bitcast.11), channel_id=1, replica_groups=mesh['slab'=4,'freq'=64] {'slab','freq'}, dimensions={0} | all-to-all | bytes 524288 | tf_op jit(solution)/shard_map/all_to_all | solution.py:418
  104.2 1.7 %last.1 = f32[32,4,1024]{2,1,0:T(4,128)} custom-call(bf16[1024,128]{1,0:T(8,128)(2,1)S(1)} %bitcast.8, bf16[1536,256]{1,0:T(8,128)(2,1)S(1)} %copy-done, bf16[1536,256]{1,0:T(8,128)(2,1)S(1)} %copy-done.1), custom_call_target="tpu_custom_call" | custom-call | flops 536870912 | bytes 4194304 | tf_op jit(solution)/shard_map/last/pallas_call | solution.py:404
  (16 shorter events, 0.0 us)
Async XLA Ops:
  1.9 12.1 %collective-permute-start.3 = (s16[272,128]{1,0:T(8,128)(2,1)}, s16[272,128]{1,0:T(8,128)(2,1)S(1)}, u32[]{:S(2)}, u32[]{:S(2)}) collective-permute-start(s16[272,128]{1,0:T(8,128)(2,1)} %get-tuple-element.28), channel_id=1, source_target_pairs={{0,64},{64,128},{128,192},{192,0},{1,65},{65,129},{129,193},{193,1... | collective-permute-start | bytes 208904 | tf_op jit(solution)/shard_map/ppermute | solution.py:425
  4.0 11.8 %collective-permute-start.4 = (s16[272,128]{1,0:T(8,128)(2,1)}, s16[272,128]{1,0:T(8,128)(2,1)S(1)}, u32[]{:S(2)}, u32[]{:S(2)}) collective-permute-start(s16[272,128]{1,0:T(8,128)(2,1)} %get-tuple-element.29), channel_id=1, source_target_pairs={{0,128},{64,192},{128,0},{192,64},{1,129},{65,193},{129,1},{193,65... | collective-permute-start | bytes 208904 | tf_op jit(solution)/shard_map/ppermute | solution.py:425
  6.6 9.2 %collective-permute-start.5 = (s16[272,128]{1,0:T(8,128)(2,1)}, s16[272,128]{1,0:T(8,128)(2,1)S(1)}, u32[]{:S(2)}, u32[]{:S(2)}) collective-permute-start(s16[272,128]{1,0:T(8,128)(2,1)} %get-tuple-element.30), channel_id=1, source_target_pairs={{0,192},{64,0},{128,64},{192,128},{1,193},{65,1},{129,65},{193,129... | collective-permute-start | bytes 208904 | tf_op jit(solution)/shard_map/ppermute | solution.py:425
  9.6 10.2 %collective-permute-start = (s16[272,128]{1,0:T(8,128)(2,1)}, s16[272,128]{1,0:T(8,128)(2,1)S(1)}, u32[]{:S(2)}, u32[]{:S(2)}) collective-permute-start(s16[272,128]{1,0:T(8,128)(2,1)} %get-tuple-element.24), channel_id=1, source_target_pairs={{0,64},{64,128},{128,192},{192,0},{1,65},{65,129},{129,193},{193,1... | collective-permute-start | bytes 208904 | tf_op jit(solution)/shard_map/ppermute | solution.py:425
  10.0 4.1 %copy-start.7 = (s16[272,128]{1,0:T(8,128)(2,1)S(1)}, s16[272,128]{1,0:T(8,128)(2,1)}, u32[]{:S(2)}) copy-start(s16[272,128]{1,0:T(8,128)(2,1)} %get-tuple-element.26) | copy-start | bytes 208900
  10.0 5.9 %copy-start.3 = (f32[2,2,32,256]{3,2,1,0:T(8,128)S(1)}, f32[2,2,32,256]{3,2,1,0:T(8,128)}, u32[]{:S(2)}) copy-start(f32[2,2,32,256]{3,2,1,0:T(8,128)} %get-tuple-element.27.own) | copy-start | bytes 393220
  10.0 5.9 %copy-start.4 = (s32[3]{0:T(128)S(1)}, s32[3]{0:T(128)}, u32[]{:S(2)}) copy-start(s32[3]{0:T(128)} %offsets_ref.5) | copy-start | bytes 40
  10.0 9.8 %collective-permute-start.1 = (s16[272,128]{1,0:T(8,128)(2,1)}, s16[272,128]{1,0:T(8,128)(2,1)S(1)}, u32[]{:S(2)}, u32[]{:S(2)}) collective-permute-start(s16[272,128]{1,0:T(8,128)(2,1)} %get-tuple-element.25), channel_id=1, source_target_pairs={{0,128},{64,192},{128,0},{192,64},{1,129},{65,193},{129,1},{193,65... | collective-permute-start | bytes 208904 | tf_op jit(solution)/shard_map/ppermute | solution.py:425
  14.0 5.8 %copy-start.2 = (f32[2,2,32,256]{3,2,1,0:T(8,128)S(1)}, f32[2,2,32,256]{3,2,1,0:T(8,128)}, u32[]{:S(2)}) copy-start(f32[2,2,32,256]{3,2,1,0:T(8,128)} %get-tuple-element.32.own) | copy-start | bytes 393220
  14.0 5.7 %collective-permute-start.2 = (s16[272,128]{1,0:T(8,128)(2,1)S(1)}, s16[272,128]{1,0:T(8,128)(2,1)S(1)}, u32[]{:S(2)}, u32[]{:S(2)}) collective-permute-start(s16[272,128]{1,0:T(8,128)(2,1)S(1)} %copy-done.7), channel_id=1, source_target_pairs={{0,192},{64,0},{128,64},{192,128},{1,193},{65,1},{129,65},{193,129... | collective-permute-start | bytes 208904 | tf_op jit(solution)/shard_map/ppermute | solution.py:425
  15.8 39.4 %copy-start = (bf16[1536,256]{1,0:T(8,128)(2,1)S(1)}, bf16[1536,256]{1,0:T(8,128)(2,1)}, u32[]{:S(2)}) copy-start(bf16[1536,256]{1,0:T(8,128)(2,1)} %constant.19.clone.angles_ref.high_ref) | copy-start | bytes 2359300
  15.8 39.4 %copy-start.5 = (bf16[512,512]{1,0:T(8,128)(2,1)S(1)}, bf16[512,512]{1,0:T(8,128)(2,1)}, u32[]{:S(2)}) copy-start(bf16[512,512]{1,0:T(8,128)(2,1)} %constant.21.clone.odd_ref) | copy-start | bytes 1572868
  15.9 39.3 %copy-start.6 = (bf16[512,256]{1,0:T(8,128)(2,1)S(1)}, bf16[512,256]{1,0:T(8,128)(2,1)}, u32[]{:S(2)}) copy-start(bf16[512,256]{1,0:T(8,128)(2,1)} %constant.20.clone.even_ref) | copy-start | bytes 786436
  55.2 49.0 %copy-start.1 = (bf16[1536,256]{1,0:T(8,128)(2,1)S(1)}, bf16[1536,256]{1,0:T(8,128)(2,1)}, u32[]{:S(2)}) copy-start(bf16[1536,256]{1,0:T(8,128)(2,1)} %constant.22.clone.low_ref) | copy-start | bytes 2359300
  56.9 20.7 %all-to-all-start.1 = ((bf16[256,4,128]{2,1,0:T(4,128)(2,1)}), bf16[256,4,128]{2,1,0:T(4,128)(2,1)S(1)}, u32[]{:S(2)}, u32[]{:S(2)}) async-start(bf16[256,4,128]{2,1,0:T(4,128)(2,1)} %bitcast.4), calls=%async_computation.1 | async-start | bytes 524288 | tf_op jit(solution)/shard_map/all_to_all | solution.py:418

commit v2 on v1

--- a/solution.py
+++ b/solution.py
@@ -60,7 +60,7 @@
 
 PARAMS = pltpu.CompilerParams(vmem_limit_bytes=20 << 20)
 ALONE = pltpu.CompilerParams(vmem_limit_bytes=100 << 19)
-SPECTRUM = jax.ShapeDtypeStruct((2, R, Z), F32)
+SPECTRUM = jax.ShapeDtypeStruct((2, 2, R, Z), F32)
 PACKED = jax.ShapeDtypeStruct((4 * Q, Z), BF16)
 
 
@@ -113,39 +113,34 @@
     return jnp.round(values * (LEVELS * jnp.exp2(-power))).astype(jnp.int32), power
 
 
-def arrange_kernel(slab_ref, initial_ref, measured_ref, own_ref, *piece_refs):
-    slab = slab_ref[0]
+def arrange_kernel(initial_ref, measured_ref, piece_ref):
     row = lax.broadcasted_iota(jnp.int32, (16, Z), 0)
+    head = jnp.zeros((16, Z), jnp.int32)
     for array, source in enumerate((initial_ref, measured_ref)):
         for part in range(2):
-            own_ref[array, part] = source[part, slab]
-    for distance, piece_ref in enumerate(piece_refs, 1):
-        index = lax.rem(slab + distance, SLABS)
-        head = jnp.zeros((16, Z), jnp.int32)
-        for array, source in enumerate((initial_ref, measured_ref)):
-            for part in range(2):
-                block = 2 * array + part
-                codes, power = encode(source[part, index])
+            for half in range(2):
+                block = 4 * half + 2 * array + part
+                codes, power = encode(source[part, half, 0])
                 codes = codes.astype(jnp.int16)
-                piece_ref[pl.ds(64 * block, 32), :] = codes[:, :Z]
-                piece_ref[pl.ds(64 * block + 32, 32), :] = codes[:, Z:]
+                piece_ref[0, pl.ds(64 * block, 32), :] = codes[:, :Z]
+                piece_ref[0, pl.ds(64 * block + 32, 32), :] = codes[:, Z:]
                 head = jnp.where(row == block, power.astype(jnp.int32), head)
-        piece_ref[pl.ds(256, 16), :] = head.astype(jnp.int16)
-
-
-def arrange(slab, initial, measured, half):
-    block = pl.BlockSpec((2, SLABS, 32, R), lambda i: (0, half, 0, 0))
-    piece = jax.ShapeDtypeStruct((272, Z), jnp.int16)
+    piece_ref[0, pl.ds(512, 16), :] = head.astype(jnp.int16)
+
+
+def arrange(initial, measured):
+    shape = (2, 2, SLABS, 32, R)
+    block = pl.BlockSpec((2, 2, 1, 32, R), lambda d: (0, 0, d, 0, 0))
     return pl.pallas_call(
         arrange_kernel,
-        grid=(1,),
-        out_shape=(jax.ShapeDtypeStruct((2, 2, 32, R), F32),) + (piece,) * 3,
-        in_specs=[SMEM, block, block],
-        out_specs=(VMEM,) * 4,
+        grid=(SLABS,),
+        out_shape=jax.ShapeDtypeStruct((SLABS, 528, Z), jnp.int16),
+        in_specs=[block, block],
+        out_specs=pl.BlockSpec((1, 528, Z), lambda d: (d, 0, 0)),
         compiler_params=pltpu.CompilerParams(vmem_limit_bytes=123 << 19),
         cost_estimate=cost(1 << 20, 1 << 20),
         name="arrange",
-    )(slab, initial, measured)
+    )(initial.reshape(shape), measured.reshape(shape))
 
 
 def moved(values, offset, lane):
@@ -185,19 +180,25 @@
             shifted[index, rows, :Z] = moved(real, offset, lane)
             shifted[index, rows, Z:] = moved(imag, offset, lane)
 
+    def product(kind, index):
+        by_real = dot(projectors[index][kind], shifted[index])
+        by_imag = dot(projectors[index][kind + 1], shifted[index])
+        return by_real, by_imag
+
+    both = range(len(projectors))
+
     def step(count, carry):
-        for index, blocks in enumerate(projectors):
-            iterate, measured = iterates[index], measures[index]
-            place(1, index, iterate[0], iterate[1])
-            by_real = dot(blocks[0], shifted[index])
-            by_imag = dot(blocks[1], shifted[index])
-            real = measured[0] - (by_real[:, :Z] - by_imag[:, Z:])
-            imag = measured[1] - (by_imag[:, :Z] + by_real[:, Z:])
+        for index in both:
+            place(1, index, iterates[index][0], iterates[index][1])
+        products = [product(0, index) for index in both]
+        for index, (by_real, by_imag) in zip(both, products):
+            real = measures[index][0] - (by_real[:, :Z] - by_imag[:, Z:])
+            imag = measures[index][1] - (by_imag[:, :Z] + by_real[:, Z:])
             place(-1, index, real.astype(BF16).astype(F32), imag.astype(BF16).astype(F32))
-            by_real = dot(blocks[2], shifted[index])
-            by_imag = dot(blocks[3], shifted[index])
-            iterate[0] += STEP_SIZE * (by_real[:, :Z] + by_imag[:, Z:])
-            iterate[1] += STEP_SIZE * (by_real[:, Z:] - by_imag[:, :Z])
+        products = [product(2, index) for index in both]
+        for index, (by_real, by_imag) in zip(both, products):
+            iterates[index][0] += STEP_SIZE * (by_real[:, :Z] + by_imag[:, Z:])
+            iterates[index][1] += STEP_SIZE * (by_real[:, Z:] - by_imag[:, :Z])
         return carry
 
     lax.fori_loop(0, INNER, step, 0)
@@ -225,109 +226,93 @@
     return copies
 
 
-def gather(slab_ref, own, pieces, column, iterate, measured):
-    slab = slab_ref[0]
-    scales = [
-        jnp.exp2(piece[pl.ds(256, 16), :].astype(jnp.int32).astype(F32)) * (1.0 / LEVELS)
-        for piece in pieces
-    ]
-    for array, target in ((0, iterate), (1, measured)):
-        for part in range(2):
-            block = 2 * array + part
-            column[pl.ds(pl.multiple_of(32 * slab, 32), 32), :] = own[array, part]
-            for distance, (piece, scale) in enumerate(zip(pieces, scales), 1):
-                rows = pl.ds(pl.multiple_of(32 * lax.rem(slab + 4 - distance, 4), 32), 32)
-                for side in range(2):
-                    codes = piece[pl.ds(64 * block + 32 * side, 32), :].astype(jnp.int32)
-                    column[rows, Z * side : Z * (side + 1)] = codes.astype(F32) * scale[block : block + 1]
-            target[part] = column[...].T
-
-
-def early_kernel(
-    slab_ref, offsets_ref, own, one, two, three, blocks_far,
-    iterate, measured, column, shifted, blocks, sems,
+def gather(pieces, column, iterate, measured):
+    for slab in range(SLABS):
+        power = pieces[slab, pl.ds(512, 16), :].astype(jnp.int32).astype(F32)
+        scale = jnp.exp2(power) * (1.0 / LEVELS)
+        for block in range(8):
+            for side in range(2):
+                codes = pieces[slab, pl.ds(64 * block + 32 * side, 32), :].astype(jnp.int32)
+                rows = pl.ds(32 * slab, 32)
+                column[block, rows, Z * side : Z * (side + 1)] = codes.astype(F32) * scale[block : block + 1]
+    for half in range(2):
+        for part in range(2):
+            iterate[half, part] = column[4 * half + part].T
+            measured[half, part] = column[4 * half + 2 + part].T
+
+
+def first_kernel(
+    offsets_ref, pieces, blocks_far,
+    iterate, measured, packed_ref, column, rows_ref, shifted, blocks, sems,
 ):
-    copies = load_blocks(blocks_far, blocks, sems, (0,))
-    gather(slab_ref, own, (one, two, three), column, iterate, measured)
+    copies = load_blocks(blocks_far, blocks, sems, (0, 1))
+    gather(pieces, column, iterate, measured)
     for copy in copies:
         copy.wait()
-    passes(offsets_ref, [blocks.at[0]], [iterate], [measured], shifted)
-
-
-def late_kernel(
-    slab_ref, offsets_ref, own, one, two, three, blocks_far, other,
-    iterate, measured, packed_ref, column, shifted, blocks, sems, rows_ref,
-):
-    copies = load_blocks(blocks_far, blocks, sems, (1,))
-    gather(slab_ref, own, (one, two, three), column, iterate, measured)
-    for copy in copies:
-        copy.wait()
-    passes(offsets_ref, [blocks.at[0]], [iterate], [measured], shifted)
-    pack([other, iterate], rows_ref, packed_ref)
+    halves = range(2)
+    iterates = [iterate.at[half] for half in halves]
+    passes(offsets_ref, [blocks.at[h] for h in halves], iterates, [measured.at[h] for h in halves], shifted)
+    pack(iterates, rows_ref, packed_ref)
 
 
 def second_kernel(
-    silent_ref, offsets_ref, packed_in, kept_0, kept_1, measured_0, measured_1, blocks_far,
-    packed_ref, iterate, shifted, rows_ref, blocks, sems,
+    silent_ref, offsets_ref, packed_in, kept, measured, blocks_far,
+    packed_ref, iterate, rows_ref, shifted, blocks, sems,
 ):
     copies = load_blocks(blocks_far, blocks, sems, (0, 1))
     rows_ref[...] = packed_in[...].astype(F32)
     silent = silent_ref[0] != 0
-    for half, kept in enumerate((kept_0, kept_1)):
+    for half in range(2):
         for part in range(2):
             parts = [
                 rows_ref[pl.ds(Q * slab + 2 * half + part, GROUPS, stride=4), :] for slab in range(4)
             ]
             for i, added in enumerate(swap_blocks(parts)):
                 rows = pl.ds(i, GROUPS, stride=4)
-                base = kept[part, rows, :]
+                base = kept[half, part, rows, :]
                 if half == 0 and part == 1:
                     base = jnp.where(silent, 0.0, base)
                 iterate[half, part, rows, :] = base + added
     for copy in copies:
         copy.wait()
     iterates = [iterate.at[0], iterate.at[1]]
-    passes(offsets_ref, [blocks.at[0], blocks.at[1]], iterates, [measured_0, measured_1], shifted)
+    measures = [measured.at[0], measured.at[1]]
+    passes(offsets_ref, [blocks.at[0], blocks.at[1]], iterates, measures, shifted)
     pack(iterates, rows_ref, packed_ref)
 
 
-def pass_scratch(halves, sems):
-    return [
-        pltpu.VMEM((halves, 3 * R, 2 * Z), BF16),
-        pltpu.VMEM((halves, 4, R, 3 * R), BF16),
-        pltpu.SemaphoreType.DMA((sems,)),
-    ]
-
-
-ROWS = pltpu.VMEM((4 * Q, Z), F32)
-
-
-def first_half(slab, offsets, pieces, blocks, other):
-    late = other is not None
-    return pl.pallas_call(
-        late_kernel if late else early_kernel,
-        out_shape=(SPECTRUM, SPECTRUM) + ((PACKED,) if late else ()),
-        in_specs=[SMEM, SMEM] + [VMEM] * 4 + [HBM] + ([VMEM] if late else []),
-        out_specs=(VMEM,) * (3 if late else 2),
-        scratch_shapes=[pltpu.VMEM((Z, R), F32)] + pass_scratch(1, 2) + ([ROWS] if late else []),
+PASS_SCRATCH = [
+    pltpu.VMEM((4 * Q, Z), F32),
+    pltpu.VMEM((2, 3 * R, 2 * Z), BF16),
+    pltpu.VMEM((2, 4, R, 3 * R), BF16),
+    pltpu.SemaphoreType.DMA((4,)),
+]
+
+
+def first_half(offsets, pieces, blocks):
+    return pl.pallas_call(
+        first_kernel,
+        out_shape=(SPECTRUM, SPECTRUM, PACKED),
+        in_specs=[SMEM, VMEM, HBM],
+        out_specs=(VMEM,) * 3,
+        scratch_shapes=[pltpu.VMEM((8, Z, R), F32)] + PASS_SCRATCH,
         compiler_params=ALONE,
-        cost_estimate=cost(1 << 30, 4 << 20),
-        name="late" if late else "early",
-    )(slab, offsets, *pieces, blocks, *((other,) if late else ()))
-
-
-def later_half(silent, offsets, packed, kept, measures, blocks):
-    shifted, held, sems = pass_scratch(2, 4)
+        cost_estimate=cost(2 << 30, 8 << 20),
+        name="first_half",
+    )(offsets, pieces, blocks)
+
+
+def later_half(silent, offsets, packed, kept, measured, blocks):
     return pl.pallas_call(
         second_kernel,
         out_shape=PACKED,
-        in_specs=[SMEM, SMEM] + [VMEM] * 5 + [HBM],
+        in_specs=[SMEM, SMEM] + [VMEM] * 3 + [HBM],
         out_specs=VMEM,
-        scratch_shapes=[pltpu.VMEM((2, 2, R, Z), F32), shifted, ROWS, held, sems],
+        scratch_shapes=[pltpu.VMEM((2, 2, R, Z), F32)] + PASS_SCRATCH,
         compiler_params=ALONE,
         cost_estimate=cost(2 << 30, 8 << 20),
         name="later_half",
-    )(silent, offsets, packed, *kept, *measures, blocks)
+    )(silent, offsets, packed, kept, measured, blocks)
 
 
 def to_volume(packed_ref, tables_ref, volume):
@@ -418,27 +403,16 @@
     return lax.all_to_all(blocks, ("slab", "freq"), 0, 0, tiled=True).reshape(packed.shape)
 
 
-def spread(slab, initial, measured, half):
-    own, *pieces = arrange(slab, initial, measured, half)
-    for distance, piece in enumerate(pieces, 1):
-        pairs = [(i, (i + distance) % SLABS) for i in range(SLABS)]
-        pieces[distance - 1] = lax.ppermute(piece, "slab", pairs)
-    return [own, *pieces]
-
-
 def on_device(initial, measured, projector, offsets):
     (angles, angles_low), (even, _), (odd, _) = tables()
     slab = lax.axis_index("slab").astype(jnp.int32)
     group = lax.axis_index("freq").astype(jnp.int32)
     silent = ((slab == 0) & (group == 0)).astype(jnp.int32).reshape(1)
-    slab = slab.reshape(1)
-    pieces = [spread(slab, initial, measured, half) for half in range(2)]
-    blocks = prepare(slab, projector)
-    kept_0, measured_0 = first_half(slab, offsets, pieces[0], blocks, None)
-    late, kept_0 = lax.optimization_barrier((pieces[1], kept_0))
-    kept_1, measured_1, packed = first_half(slab, offsets, late, blocks, kept_0)
+    pieces = lax.all_to_all(arrange(initial, measured), "slab", 0, 0, tiled=True)
+    blocks = prepare(slab.reshape(1), projector)
+    kept, measured, packed = first_half(offsets, pieces, blocks)
     packed = exchange(middle(exchange(packed), angles, even, odd))
-    packed = later_half(silent, offsets, packed, (kept_0, kept_1), (measured_0, measured_1), blocks)
+    packed = later_half(silent, offsets, packed, kept, measured, blocks)
     return last(exchange(packed), angles, angles_low)
 
 

time: 106 us -> 102 us (0.962)
  waiting for transfers between devices: 15.3 us -> 19.9 us
  Pallas kernels: 24.9 us -> 20.9 us
  starting transfers between devices: 14.1 us -> 10.2 us
    ppermute x6 -> x0, starting transfers between devices: 8.77 us -> none  [spread(): pieces[distance - 1] = lax.ppermute(piece, 'slab', pairs)]
    all_to_all x0 -> x1, starting transfers between devices: none -> 5 us  [on_device(): lax.all_to_all(arrange(initial, measured), 'slab', 0, 0, tiled=True)]
    all_to_all x0 -> x1, waiting for transfers between devices: none -> 4.51 us  [on_device(): lax.all_to_all(arrange(initial, measured), 'slab', 0, 0, tiled=True)]
    pallas_call x4 -> x2, Pallas kernels: 12 us -> 8.9 us  [the longest x1 5.32 us: first_half(): pl.pallas_call(first_kernel, out_shape=(SPECTRUM, SPECTRUM, PACKED), in_s...]
  transfers between devices with their start and end apart: 7 -> 2, of which waited for: 1 -> 2; matrix products, arithmetic and copies ran while one was open for 0% -> 0% of each run, Pallas kernels for 8% -> 3%
where the time goes in v2:
time: 102 us
  blocking collectives  50.6 us (50%)
  Pallas kernels  20.9 us (20%)
  waiting for transfers between devices  19.9 us (20%)
  starting transfers between devices  10.2 us (10%)
    all_to_all x2, blocking collectives, exchange(): lax.all_to_all(blocks, ('slab', 'freq'), 0, 0, tiled=True)  50.6 us
    all_to_all x1, waiting for transfers between devices, exchange(): lax.all_to_all(blocks, ('slab', 'freq'), 0, 0, tiled=True)  15.4 us
    pallas_call x1, Pallas kernels, later_half(): pl.pallas_call(second_kernel, out_shape=PACKED, in_specs=[SMEM, SMEM] + [...  5.34 us
    pallas_call x1, Pallas kernels, first_half(): pl.pallas_call(first_kernel, out_shape=(SPECTRUM, SPECTRUM, PACKED), in_s...  5.32 us
    all_to_all x1, starting transfers between devices, exchange(): lax.all_to_all(blocks, ('slab', 'freq'), 0, 0, tiled=True)  5.25 us
    all_to_all x1, starting transfers between devices, on_device(): lax.all_to_all(arrange(initial, measured), 'slab', 0, 0, tiled=True)  5 us
    all_to_all x1, waiting for transfers between devices, on_device(): lax.all_to_all(arrange(initial, measured), 'slab', 0, 0, tiled=True)  4.51 us
    pallas_call x1, Pallas kernels, arrange(): pl.pallas_call(arrange_kernel, grid=(SLABS,), out_shape=jax.ShapeDtypeStr...  3.58 us
  transfers between devices with their start and end apart: 2, of which 2 were waited for; matrix products, arithmetic and copies ran while one was open for 0% of the time, Pallas kernels for 3%

profile of v2, /device:TPU:1, one launch (start us, length us, event | category | flops | bytes accessed | tf_op | source)
XLA Modules:
  0.0 101.8 jit_solution(6311705960706015870)
XLA Ops:
  0.0 3.6 %arrange.1 = s16[4,528,128]{2,1,0:T(8,128)(2,1)} custom-call(f32[2,2,4,32,256]{4,3,2,1,0:T(8,128)} %bitcast.15, f32[2,2,4,32,256]{4,3,2,1,0:T(8,128)} %bitcast.16), custom_call_target="tpu_custom_call" | custom-call | flops 1048576 | bytes 1048576 | tf_op jit(solution)/shard_map/arrange/pallas_call | solution.py:134
  3.6 5.0 %all-to-all-start = ((s16[4,528,128]{2,1,0:T(8,128)(2,1)}), s16[4,528,128]{2,1,0:T(8,128)(2,1)S(1)}, u32[]{:S(2)}, u32[]{:S(2)}) async-start(s16[4,528,128]{2,1,0:T(8,128)(2,1)} %arrange.1), calls=%async_computation | async-start | bytes 1081344 | tf_op jit(solution)/shard_map/all_to_all | solution.py:411
  8.6 0.0 copy-start.2
  8.6 3.3 %prepare.1.blocks_far = bf16[4,4,256,768]{3,2,1,0:T(8,128)(2,1)} custom-call(s32[1]{0:T(128)} %bitcast.3.slab_ref, bf16[3,2,8,256,256]{4,3,2,1,0:T(8,128)(2,1)} %projector_ref.1), custom_call_target="tpu_custom_call" | custom-call | bytes 8388608 | tf_op jit(solution)/shard_map/prepare/pallas_call | solution.py:98
  11.8 0.0 copy-start
  11.9 0.0 copy-start.3
  11.9 0.0 copy-start.4
  11.9 4.5 %all-to-all-done.pieces = s16[4,528,128]{2,1,0:T(8,128)(2,1)S(1)} async-done(((s16[4,528,128]{2,1,0:T(8,128)(2,1)}), s16[4,528,128]{2,1,0:T(8,128)(2,1)S(1)}, u32[]{:S(2)}, u32[]{:S(2)}) %all-to-all-start) | async-done | bytes 540704 | tf_op jit(solution)/shard_map/all_to_all | solution.py:411
  16.4 0.0 copy-done.2
  16.4 5.3 %first_half.1 = (f32[2,2,256,128]{3,2,1,0:T(8,128)S(1)}, f32[2,2,256,128]{3,2,1,0:T(8,128)S(1)}, bf16[1024,128]{1,0:T(8,128)(2,1)S(1)}) custom-call(s32[3]{0:T(128)S(1)} %copy-done.2, s16[4,528,128]{2,1,0:T(8,128)(2,1)S(1)} %all-to-all-done.pieces, bf16[4,4,256,768]{3,2,1,0:T(8,128)(2,1)} %prepare.1.blocks_far), custom_call_target="tpu_custom_call" | custom-call | flops 2147483648 | bytes 8388608 | tf_op jit(solution)/shard_map/first_half/pallas_call | solution.py:293
  21.7 30.2 %all_to_all.20 = bf16[256,4,128]{2,1,0:T(4,128)(2,1)S(1)} all-to-all(bf16[256,4,128]{2,1,0:T(4,128)(2,1)S(1)} %bitcast.13), channel_id=1, replica_groups=mesh['slab'=4,'freq'=64] {'slab','freq'}, dimensions={0} | all-to-all | bytes 524288 | tf_op jit(solution)/shard_map/all_to_all | solution.py:403
  51.9 0.0 copy-done
  51.9 0.0 copy-done.3
  51.9 0.0 copy-done.4
  51.9 0.0 copy-start.1
  51.9 1.7 %middle.1 = bf16[1024,128]{1,0:T(8,128)(2,1)} custom-call(bf16[1024,128]{1,0:T(8,128)(2,1)S(1)} %bitcast.14, bf16[1536,256]{1,0:T(8,128)(2,1)S(1)} %copy-done, bf16[512,256]{1,0:T(8,128)(2,1)S(1)} %copy-done.4, bf16[512,512]{1,0:T(8,128)(2,1)S(1)} %copy-done.3), custom_call_target="tpu_custom_call" | custom-call | flops 1073741824 | bytes 4194304 | tf_op jit(solution)/shard_map/middle/pallas_call | solution.py:367
  53.7 5.2 %all-to-all-start.2 = ((bf16[256,4,128]{2,1,0:T(4,128)(2,1)}), bf16[256,4,128]{2,1,0:T(4,128)(2,1)S(1)}, u32[]{:S(2)}, u32[]{:S(2)}) async-start(bf16[256,4,128]{2,1,0:T(4,128)(2,1)} %bitcast.6), calls=%async_computation.2 | async-start | bytes 524288 | tf_op jit(solution)/shard_map/all_to_all | solution.py:403
  58.9 15.4 %all-to-all-done.2 = bf16[256,4,128]{2,1,0:T(4,128)(2,1)S(1)} async-done(((bf16[256,4,128]{2,1,0:T(4,128)(2,1)}), bf16[256,4,128]{2,1,0:T(4,128)(2,1)S(1)}, u32[]{:S(2)}, u32[]{:S(2)}) %all-to-all-start.2) | async-done | bytes 262176 | tf_op jit(solution)/shard_map/all_to_all | solution.py:403
  74.3 5.3 %later_half.1 = bf16[1024,128]{1,0:T(8,128)(2,1)S(1)} custom-call(s32[1]{0:T(128)} %bitcast.silent_ref, s32[3]{0:T(128)S(1)} %copy-done.2, bf16[1024,128]{1,0:T(8,128)(2,1)S(1)} %bitcast.11, f32[2,2,256,128]{3,2,1,0:T(8,128)S(1)} %get-tuple-element.9.kept, f32[2,2,256,128]{3,2,1,0:T(8,128)S(1)} %get-tuple-element.10.measured, ...), custom_call_target="tpu_custom_call" | custom-call | flops 2147483648 | bytes 8388608 | tf_op jit(solution)/shard_map/later_half/pallas_call | solution.py:306
  79.7 20.4 %all_to_all.21 = bf16[256,4,128]{2,1,0:T(4,128)(2,1)S(1)} all-to-all(bf16[256,4,128]{2,1,0:T(4,128)(2,1)S(1)} %bitcast.12), channel_id=1, replica_groups=mesh['slab'=4,'freq'=64] {'slab','freq'}, dimensions={0} | all-to-all | bytes 524288 | tf_op jit(solution)/shard_map/all_to_all | solution.py:403
  100.1 0.0 copy-done.1
  100.1 1.7 %last.1 = f32[32,4,1024]{2,1,0:T(4,128)} custom-call(bf16[1024,128]{1,0:T(8,128)(2,1)S(1)} %bitcast.10, bf16[1536,256]{1,0:T(8,128)(2,1)S(1)} %copy-done, bf16[1536,256]{1,0:T(8,128)(2,1)S(1)} %copy-done.1), custom_call_target="tpu_custom_call" | custom-call | flops 536870912 | bytes 4194304 | tf_op jit(solution)/shard_map/last/pallas_call | solution.py:389
Async XLA Ops:
  3.6 12.8 %all-to-all-start = ((s16[4,528,128]{2,1,0:T(8,128)(2,1)}), s16[4,528,128]{2,1,0:T(8,128)(2,1)S(1)}, u32[]{:S(2)}, u32[]{:S(2)}) async-start(s16[4,528,128]{2,1,0:T(8,128)(2,1)} %arrange.1), calls=%async_computation | async-start | bytes 1081344 | tf_op jit(solution)/shard_map/all_to_all | solution.py:411
  8.6 7.8 %copy-start.2 = (s32[3]{0:T(128)S(1)}, s32[3]{0:T(128)}, u32[]{:S(2)}) copy-start(s32[3]{0:T(128)} %offsets_ref.3) | copy-start | bytes 40
  11.8 40.1 %copy-start = (bf16[1536,256]{1,0:T(8,128)(2,1)S(1)}, bf16[1536,256]{1,0:T(8,128)(2,1)}, u32[]{:S(2)}) copy-start(bf16[1536,256]{1,0:T(8,128)(2,1)} %constant.19.clone.angles_ref.high_ref) | copy-start | bytes 2359300
  11.9 40.0 %copy-start.3 = (bf16[512,512]{1,0:T(8,128)(2,1)S(1)}, bf16[512,512]{1,0:T(8,128)(2,1)}, u32[]{:S(2)}) copy-start(bf16[512,512]{1,0:T(8,128)(2,1)} %constant.21.clone.odd_ref) | copy-start | bytes 1572868
  11.9 40.0 %copy-start.4 = (bf16[512,256]{1,0:T(8,128)(2,1)S(1)}, bf16[512,256]{1,0:T(8,128)(2,1)}, u32[]{:S(2)}) copy-start(bf16[512,256]{1,0:T(8,128)(2,1)} %constant.20.clone.even_ref) | copy-start | bytes 786436
  51.9 48.2 %copy-start.1 = (bf16[1536,256]{1,0:T(8,128)(2,1)S(1)}, bf16[1536,256]{1,0:T(8,128)(2,1)}, u32[]{:S(2)}) copy-start(bf16[1536,256]{1,0:T(8,128)(2,1)} %constant.22.clone.low_ref) | copy-start | bytes 2359300
  53.7 20.7 %all-to-all-start.2 = ((bf16[256,4,128]{2,1,0:T(4,128)(2,1)}), bf16[256,4,128]{2,1,0:T(4,128)(2,1)S(1)}, u32[]{:S(2)}, u32[]{:S(2)}) async-start(bf16[256,4,128]{2,1,0:T(4,128)(2,1)} %bitcast.6), calls=%async_computation.2 | async-start | bytes 524288 | tf_op jit(solution)/shard_map/all_to_all | solution.py:403

commit v3 on v2

--- a/solution.py
+++ b/solution.py
@@ -113,34 +113,52 @@
     return jnp.round(values * (LEVELS * jnp.exp2(-power))).astype(jnp.int32), power
 
 
-def arrange_kernel(initial_ref, measured_ref, piece_ref):
+def arrange_kernel(initial_ref, measured_ref, pieces_ref, source, pieces, sems):
+    loads, stores = [], []
+    for chunk in range(4):
+        far = (initial_ref, measured_ref)[chunk // 2].at[chunk % 2]
+        loads.append(pltpu.make_async_copy(far, source.at[chunk], sems.at[chunk]))
+        loads[-1].start()
     row = lax.broadcasted_iota(jnp.int32, (16, Z), 0)
-    head = jnp.zeros((16, Z), jnp.int32)
-    for array, source in enumerate((initial_ref, measured_ref)):
-        for part in range(2):
+    heads = [jnp.zeros((16, Z), jnp.int32)] * SLABS
+    for chunk in range(4):
+        loads[chunk].wait()
+        for slab in range(SLABS):
             for half in range(2):
-                block = 4 * half + 2 * array + part
-                codes, power = encode(source[part, half, 0])
+                block = 2 * chunk + half
+                codes, power = encode(source[chunk, slab + 4 * half])
                 codes = codes.astype(jnp.int16)
-                piece_ref[0, pl.ds(64 * block, 32), :] = codes[:, :Z]
-                piece_ref[0, pl.ds(64 * block + 32, 32), :] = codes[:, Z:]
-                head = jnp.where(row == block, power.astype(jnp.int32), head)
-    piece_ref[0, pl.ds(512, 16), :] = head.astype(jnp.int16)
+                pieces[slab, pl.ds(64 * block, 32), :] = codes[:, :Z]
+                pieces[slab, pl.ds(64 * block + 32, 32), :] = codes[:, Z:]
+                heads[slab] = jnp.where(row == block, power.astype(jnp.int32), heads[slab])
+        rows = pl.ds(128 * chunk, 128)
+        if chunk == 3:
+            for slab in range(SLABS):
+                pieces[slab, pl.ds(512, 16), :] = heads[slab].astype(jnp.int16)
+            rows = pl.ds(384, 144)
+        stores.append(
+            pltpu.make_async_copy(pieces.at[:, rows], pieces_ref.at[:, rows], sems.at[4 + chunk])
+        )
+        stores[-1].start()
+    for copy in stores:
+        copy.wait()
 
 
 def arrange(initial, measured):
-    shape = (2, 2, SLABS, 32, R)
-    block = pl.BlockSpec((2, 2, 1, 32, R), lambda d: (0, 0, d, 0, 0))
     return pl.pallas_call(
         arrange_kernel,
-        grid=(SLABS,),
         out_shape=jax.ShapeDtypeStruct((SLABS, 528, Z), jnp.int16),
-        in_specs=[block, block],
-        out_specs=pl.BlockSpec((1, 528, Z), lambda d: (d, 0, 0)),
-        compiler_params=pltpu.CompilerParams(vmem_limit_bytes=123 << 19),
+        in_specs=[HBM, HBM],
+        out_specs=HBM,
+        scratch_shapes=[
+            pltpu.VMEM((4, 2 * SLABS, 32, R), F32),
+            pltpu.VMEM((SLABS, 528, Z), jnp.int16),
+            pltpu.SemaphoreType.DMA((8,)),
+        ],
+        compiler_params=pltpu.CompilerParams(vmem_limit_bytes=126 << 19),
         cost_estimate=cost(1 << 20, 1 << 20),
         name="arrange",
-    )(initial.reshape(shape), measured.reshape(shape))
+    )(initial, measured)
 
 
 def moved(values, offset, lane):
@@ -170,102 +188,102 @@
     return out
 
 
-def passes(offsets_ref, projectors, iterates, measures, shifted):
+def passes(offsets_ref, blocks_far, iterate, measured, buffers, begin):
+    packed_ref, rows_ref, shifted, blocks, sems = buffers
     lane = lax.broadcasted_iota(jnp.int32, (R, Z), 1)
-
-    def place(slot_sign, index, real, imag):
+    loads = [
+        pltpu.make_async_copy(blocks_far.at[half], blocks.at[half], sems.at[half]) for half in range(2)
+    ]
+    for copy in loads:
+        copy.start()
+
+    def place(sign, half, real, imag):
         for slot in range(3):
             rows = pl.ds(R * slot, R)
-            offset = slot_sign * offsets_ref[slot]
-            shifted[index, rows, :Z] = moved(real, offset, lane)
-            shifted[index, rows, Z:] = moved(imag, offset, lane)
-
-    def product(kind, index):
-        by_real = dot(projectors[index][kind], shifted[index])
-        by_imag = dot(projectors[index][kind + 1], shifted[index])
+            offset = sign * offsets_ref[slot]
+            shifted[half, rows, :Z] = moved(real, offset, lane)
+            shifted[half, rows, Z:] = moved(imag, offset, lane)
+
+    def place_iterate(half):
+        place(1, half, iterate[half, 0], iterate[half, 1])
+
+    def product(kind, half):
+        by_real = dot(blocks[half, kind], shifted[half])
+        by_imag = dot(blocks[half, kind + 1], shifted[half])
         return by_real, by_imag
 
-    both = range(len(projectors))
-
-    def step(count, carry):
-        for index in both:
-            place(1, index, iterates[index][0], iterates[index][1])
-        products = [product(0, index) for index in both]
-        for index, (by_real, by_imag) in zip(both, products):
-            real = measures[index][0] - (by_real[:, :Z] - by_imag[:, Z:])
-            imag = measures[index][1] - (by_imag[:, :Z] + by_real[:, Z:])
-            place(-1, index, real.astype(BF16).astype(F32), imag.astype(BF16).astype(F32))
-        products = [product(2, index) for index in both]
-        for index, (by_real, by_imag) in zip(both, products):
-            iterates[index][0] += STEP_SIZE * (by_real[:, :Z] + by_imag[:, Z:])
-            iterates[index][1] += STEP_SIZE * (by_real[:, Z:] - by_imag[:, :Z])
-        return carry
-
-    lax.fori_loop(0, INNER, step, 0)
-
-
-def pack(iterates, rows_ref, packed_ref):
-    for half, iterate in enumerate(iterates):
-        for part in range(2):
-            blocks = [iterate[part, pl.ds(i, GROUPS, stride=4), :] for i in range(4)]
-            for slab, block in enumerate(swap_blocks(blocks)):
-                rows_ref[pl.ds(Q * slab + 2 * half + part, GROUPS, stride=4), :] = block
+    def place_residual(half, by_real, by_imag):
+        real = measured[half, 0] - (by_real[:, :Z] - by_imag[:, Z:])
+        imag = measured[half, 1] - (by_imag[:, :Z] + by_real[:, Z:])
+        place(-1, half, real.astype(BF16).astype(F32), imag.astype(BF16).astype(F32))
+
+    def update(half, by_real, by_imag):
+        iterate[half, 0] += STEP_SIZE * (by_real[:, :Z] + by_imag[:, Z:])
+        iterate[half, 1] += STEP_SIZE * (by_real[:, Z:] - by_imag[:, :Z])
+
+    begin(0)
+    begin(1)
+    loads[0].wait()
+    place_iterate(0)
+    place_iterate(1)
+    first = product(0, 0)
+    loads[1].wait()
+    second = product(0, 1)
+    for count in range(INNER):
+        if count:
+            first = product(0, 0)
+            second = product(0, 1)
+        place_residual(0, *first)
+        place_residual(1, *second)
+        first = product(2, 0)
+        second = product(2, 1)
+        update(0, *first)
+        update(1, *second)
+        if count + 1 < INNER:
+            place_iterate(0)
+            place_iterate(1)
+    pack(0, iterate, rows_ref)
+    pack(1, iterate, rows_ref)
     packed_ref[...] = rows_ref[...].astype(packed_ref.dtype)
 
 
-def load_blocks(blocks_far, blocks, sems, halves):
-    copies = []
-    for index, half in enumerate(halves):
-        for kind in range(2):
-            pair = pl.ds(2 * kind, 2)
-            copy = pltpu.make_async_copy(
-                blocks_far.at[half, pair], blocks.at[index, pair], sems.at[len(copies)]
-            )
-            copy.start()
-            copies.append(copy)
-    return copies
-
-
-def gather(pieces, column, iterate, measured):
+def pack(half, iterate, rows_ref):
+    for part in range(2):
+        blocks = [iterate[half, part, pl.ds(i, GROUPS, stride=4), :] for i in range(4)]
+        for slab, block in enumerate(swap_blocks(blocks)):
+            rows_ref[pl.ds(Q * slab + 2 * half + part, GROUPS, stride=4), :] = block
+
+
+def first_kernel(offsets_ref, pieces, blocks_far, iterate, measured, packed_ref, column, *scratch):
+    scales = []
     for slab in range(SLABS):
         power = pieces[slab, pl.ds(512, 16), :].astype(jnp.int32).astype(F32)
-        scale = jnp.exp2(power) * (1.0 / LEVELS)
-        for block in range(8):
-            for side in range(2):
-                codes = pieces[slab, pl.ds(64 * block + 32 * side, 32), :].astype(jnp.int32)
-                rows = pl.ds(32 * slab, 32)
-                column[block, rows, Z * side : Z * (side + 1)] = codes.astype(F32) * scale[block : block + 1]
-    for half in range(2):
-        for part in range(2):
-            iterate[half, part] = column[4 * half + part].T
-            measured[half, part] = column[4 * half + 2 + part].T
-
-
-def first_kernel(
-    offsets_ref, pieces, blocks_far,
-    iterate, measured, packed_ref, column, rows_ref, shifted, blocks, sems,
-):
-    copies = load_blocks(blocks_far, blocks, sems, (0, 1))
-    gather(pieces, column, iterate, measured)
-    for copy in copies:
-        copy.wait()
-    halves = range(2)
-    iterates = [iterate.at[half] for half in halves]
-    passes(offsets_ref, [blocks.at[h] for h in halves], iterates, [measured.at[h] for h in halves], shifted)
-    pack(iterates, rows_ref, packed_ref)
+        scales.append(jnp.exp2(power) * (1.0 / LEVELS))
+
+    def begin(half):
+        for chunk in range(4):
+            block = 2 * chunk + half
+            for slab in range(SLABS):
+                for side in range(2):
+                    codes = pieces[slab, pl.ds(64 * block + 32 * side, 32), :].astype(jnp.int32)
+                    values = codes.astype(F32) * scales[slab][block : block + 1]
+                    column[block, pl.ds(32 * slab, 32), Z * side : Z * (side + 1)] = values
+            (iterate, measured)[chunk // 2][half, chunk % 2] = column[block].T
+
+    passes(offsets_ref, blocks_far, iterate, measured, (packed_ref, *scratch), begin)
 
 
 def second_kernel(
     silent_ref, offsets_ref, packed_in, kept, measured, blocks_far,
-    packed_ref, iterate, rows_ref, shifted, blocks, sems,
+    packed_ref, arrived, iterate, *scratch,
 ):
-    copies = load_blocks(blocks_far, blocks, sems, (0, 1))
-    rows_ref[...] = packed_in[...].astype(F32)
     silent = silent_ref[0] != 0
-    for half in range(2):
+    arrived[...] = packed_in[...].astype(F32)
+
+    def begin(half):
         for part in range(2):
             parts = [
-                rows_ref[pl.ds(Q * slab + 2 * half + part, GROUPS, stride=4), :] for slab in range(4)
+                arrived[pl.ds(Q * slab + 2 * half + part, GROUPS, stride=4), :] for slab in range(4)
             ]
             for i, added in enumerate(swap_blocks(parts)):
                 rows = pl.ds(i, GROUPS, stride=4)
@@ -273,19 +291,15 @@
                 if half == 0 and part == 1:
                     base = jnp.where(silent, 0.0, base)
                 iterate[half, part, rows, :] = base + added
-    for copy in copies:
-        copy.wait()
-    iterates = [iterate.at[0], iterate.at[1]]
-    measures = [measured.at[0], measured.at[1]]
-    passes(offsets_ref, [blocks.at[0], blocks.at[1]], iterates, measures, shifted)
-    pack(iterates, rows_ref, packed_ref)
+
+    passes(offsets_ref, blocks_far, iterate, measured, (packed_ref, *scratch), begin)
 
 
 PASS_SCRATCH = [
     pltpu.VMEM((4 * Q, Z), F32),
     pltpu.VMEM((2, 3 * R, 2 * Z), BF16),
     pltpu.VMEM((2, 4, R, 3 * R), BF16),
-    pltpu.SemaphoreType.DMA((4,)),
+    pltpu.SemaphoreType.DMA((2,)),
 ]
 
 
@@ -308,7 +322,7 @@
         out_shape=PACKED,
         in_specs=[SMEM, SMEM] + [VMEM] * 3 + [HBM],
         out_specs=VMEM,
-        scratch_shapes=[pltpu.VMEM((2, 2, R, Z), F32)] + PASS_SCRATCH,
+        scratch_shapes=[pltpu.VMEM((4 * Q, Z), F32), pltpu.VMEM((2, 2, R, Z), F32)] + PASS_SCRATCH,
         compiler_params=ALONE,
         cost_estimate=cost(2 << 30, 8 << 20),
         name="later_half",

time: 102 us -> 99.1 us (0.972)
  Pallas kernels: 20.9 us -> 17.9 us
    pallas_call x1, Pallas kernels: 3.58 us -> 2.3 us  [arrange(): pl.pallas_call(arrange_kernel, out_shape=jax.ShapeDtypeStruct((SLABS, 528...]
where the time goes in v3:
time: 99.1 us; the launch traced here: 98.8 us
  blocking collectives  50.6 us (51%)
  waiting for transfers between devices  19.9 us (20%)
  Pallas kernels  17.9 us (18%)
  starting transfers between devices  10.3 us (10%)
    all_to_all x2, blocking collectives, exchange(): lax.all_to_all(blocks, ('slab', 'freq'), 0, 0, tiled=True)  50.6 us
    all_to_all x1, waiting for transfers between devices, exchange(): lax.all_to_all(blocks, ('slab', 'freq'), 0, 0, tiled=True)  15.4 us
    all_to_all x1, starting transfers between devices, exchange(): lax.all_to_all(blocks, ('slab', 'freq'), 0, 0, tiled=True)  5.25 us
    all_to_all x1, starting transfers between devices, on_device(): lax.all_to_all(arrange(initial, measured), 'slab', 0, 0, tiled=True)  5.01 us
    all_to_all x1, waiting for transfers between devices, on_device(): lax.all_to_all(arrange(initial, measured), 'slab', 0, 0, tiled=True)  4.51 us
    pallas_call x1, Pallas kernels, first_half(): pl.pallas_call(first_kernel, out_shape=(SPECTRUM, SPECTRUM, PACKED), in_s...  4.49 us
    pallas_call x1, Pallas kernels, later_half(): pl.pallas_call(second_kernel, out_shape=PACKED, in_specs=[SMEM, SMEM] + [...  4.47 us
    pallas_call x1, Pallas kernels, prepare(): pl.pallas_call(prepare_kernel, out_shape=jax.ShapeDtypeStruct((4, 4, R, 3...  3.25 us
  transfers between devices with their start and end apart: 2, of which 2 were waited for; matrix products, arithmetic and copies ran while one was open for 0% of the time, Pallas kernels for 3%

profile of v3, /device:TPU:1, one launch (start us, length us, event | category | flops | bytes accessed | tf_op | source)
XLA Modules:
  0.0 98.8 jit_solution(3516448541800563770)
XLA Ops:
  0.0 2.3 %arrange.1 = s16[4,528,128]{2,1,0:T(8,128)(2,1)} custom-call(f32[2,8,32,256]{3,2,1,0:T(8,128)} %initial_ref.1, f32[2,8,32,256]{3,2,1,0:T(8,128)} %measured_ref.1), custom_call_target="tpu_custom_call" | custom-call | flops 1048576 | bytes 1048576 | tf_op jit(solution)/shard_map/arrange/pallas_call | solution.py:148
  2.3 5.0 %all-to-all-start = ((s16[4,528,128]{2,1,0:T(8,128)(2,1)}), s16[4,528,128]{2,1,0:T(8,128)(2,1)S(1)}, u32[]{:S(2)}, u32[]{:S(2)}) async-start(s16[4,528,128]{2,1,0:T(8,128)(2,1)} %arrange.1), calls=%async_computation | async-start | bytes 1081344 | tf_op jit(solution)/shard_map/all_to_all | solution.py:425
  7.3 0.0 copy-start.2
  7.3 3.3 %prepare.1.blocks_far = bf16[4,4,256,768]{3,2,1,0:T(8,128)(2,1)} custom-call(s32[1]{0:T(128)} %bitcast.1.slab_ref, bf16[3,2,8,256,256]{4,3,2,1,0:T(8,128)(2,1)} %projector_ref.1), custom_call_target="tpu_custom_call" | custom-call | bytes 8388608 | tf_op jit(solution)/shard_map/prepare/pallas_call | solution.py:98
  10.6 0.0 copy-start
  10.6 0.0 copy-start.3
  10.6 0.0 copy-start.4
  10.6 4.5 %all-to-all-done.pieces = s16[4,528,128]{2,1,0:T(8,128)(2,1)S(1)} async-done(((s16[4,528,128]{2,1,0:T(8,128)(2,1)}), s16[4,528,128]{2,1,0:T(8,128)(2,1)S(1)}, u32[]{:S(2)}, u32[]{:S(2)}) %all-to-all-start) | async-done | bytes 540704 | tf_op jit(solution)/shard_map/all_to_all | solution.py:425
  15.1 0.0 copy-done.2
  15.1 4.5 %first_half.1 = (f32[2,2,256,128]{3,2,1,0:T(8,128)S(1)}, f32[2,2,256,128]{3,2,1,0:T(8,128)S(1)}, bf16[1024,128]{1,0:T(8,128)(2,1)S(1)}) custom-call(s32[3]{0:T(128)S(1)} %copy-done.2, s16[4,528,128]{2,1,0:T(8,128)(2,1)S(1)} %all-to-all-done.pieces, bf16[4,4,256,768]{3,2,1,0:T(8,128)(2,1)} %prepare.1.blocks_far), custom_call_target="tpu_custom_call" | custom-call | flops 2147483648 | bytes 8388608 | tf_op jit(solution)/shard_map/first_half/pallas_call | solution.py:307
  19.6 30.2 %all_to_all.20 = bf16[256,4,128]{2,1,0:T(4,128)(2,1)S(1)} all-to-all(bf16[256,4,128]{2,1,0:T(4,128)(2,1)S(1)} %bitcast.11), channel_id=1, replica_groups=mesh['slab'=4,'freq'=64] {'slab','freq'}, dimensions={0} | all-to-all | bytes 524288 | tf_op jit(solution)/shard_map/all_to_all | solution.py:417
  49.8 0.0 copy-done
  49.8 0.0 copy-done.3
  49.8 0.0 copy-done.4
  49.8 0.0 copy-start.1
  49.8 1.7 %middle.1 = bf16[1024,128]{1,0:T(8,128)(2,1)} custom-call(bf16[1024,128]{1,0:T(8,128)(2,1)S(1)} %bitcast.12, bf16[1536,256]{1,0:T(8,128)(2,1)S(1)} %copy-done, bf16[512,256]{1,0:T(8,128)(2,1)S(1)} %copy-done.4, bf16[512,512]{1,0:T(8,128)(2,1)S(1)} %copy-done.3), custom_call_target="tpu_custom_call" | custom-call | flops 1073741824 | bytes 4194304 | tf_op jit(solution)/shard_map/middle/pallas_call | solution.py:381
  51.5 5.2 %all-to-all-start.2 = ((bf16[256,4,128]{2,1,0:T(4,128)(2,1)}), bf16[256,4,128]{2,1,0:T(4,128)(2,1)S(1)}, u32[]{:S(2)}, u32[]{:S(2)}) async-start(bf16[256,4,128]{2,1,0:T(4,128)(2,1)} %bitcast.4), calls=%async_computation.2 | async-start | bytes 524288 | tf_op jit(solution)/shard_map/all_to_all | solution.py:417
  56.8 15.4 %all-to-all-done.2 = bf16[256,4,128]{2,1,0:T(4,128)(2,1)S(1)} async-done(((bf16[256,4,128]{2,1,0:T(4,128)(2,1)}), bf16[256,4,128]{2,1,0:T(4,128)(2,1)S(1)}, u32[]{:S(2)}, u32[]{:S(2)}) %all-to-all-start.2) | async-done | bytes 262176 | tf_op jit(solution)/shard_map/all_to_all | solution.py:417
  72.2 4.5 %later_half.1 = bf16[1024,128]{1,0:T(8,128)(2,1)S(1)} custom-call(s32[1]{0:T(128)} %bitcast.silent_ref, s32[3]{0:T(128)S(1)} %copy-done.2, bf16[1024,128]{1,0:T(8,128)(2,1)S(1)} %bitcast.9, f32[2,2,256,128]{3,2,1,0:T(8,128)S(1)} %get-tuple-element.9.kept, f32[2,2,256,128]{3,2,1,0:T(8,128)S(1)} %get-tuple-element.10.measured, ...), custom_call_target="tpu_custom_call" | custom-call | flops 2147483648 | bytes 8388608 | tf_op jit(solution)/shard_map/later_half/pallas_call | solution.py:320
  76.7 20.4 %all_to_all.21 = bf16[256,4,128]{2,1,0:T(4,128)(2,1)S(1)} all-to-all(bf16[256,4,128]{2,1,0:T(4,128)(2,1)S(1)} %bitcast.10), channel_id=1, replica_groups=mesh['slab'=4,'freq'=64] {'slab','freq'}, dimensions={0} | all-to-all | bytes 524288 | tf_op jit(solution)/shard_map/all_to_all | solution.py:417
  97.1 0.0 copy-done.1
  97.1 1.7 %last.1 = f32[32,4,1024]{2,1,0:T(4,128)} custom-call(bf16[1024,128]{1,0:T(8,128)(2,1)S(1)} %bitcast.8, bf16[1536,256]{1,0:T(8,128)(2,1)S(1)} %copy-done, bf16[1536,256]{1,0:T(8,128)(2,1)S(1)} %copy-done.1), custom_call_target="tpu_custom_call" | custom-call | flops 536870912 | bytes 4194304 | tf_op jit(solution)/shard_map/last/pallas_call | solution.py:403
Async XLA Ops:
  2.3 12.8 %all-to-all-start = ((s16[4,528,128]{2,1,0:T(8,128)(2,1)}), s16[4,528,128]{2,1,0:T(8,128)(2,1)S(1)}, u32[]{:S(2)}, u32[]{:S(2)}) async-start(s16[4,528,128]{2,1,0:T(8,128)(2,1)} %arrange.1), calls=%async_computation | async-start | bytes 1081344 | tf_op jit(solution)/shard_map/all_to_all | solution.py:425
  7.3 7.8 %copy-start.2 = (s32[3]{0:T(128)S(1)}, s32[3]{0:T(128)}, u32[]{:S(2)}) copy-start(s32[3]{0:T(128)} %offsets_ref.3) | copy-start | bytes 40
  10.6 39.2 %copy-start = (bf16[1536,256]{1,0:T(8,128)(2,1)S(1)}, bf16[1536,256]{1,0:T(8,128)(2,1)}, u32[]{:S(2)}) copy-start(bf16[1536,256]{1,0:T(8,128)(2,1)} %constant.19.clone.angles_ref.high_ref) | copy-start | bytes 2359300
  10.6 39.2 %copy-start.3 = (bf16[512,512]{1,0:T(8,128)(2,1)S(1)}, bf16[512,512]{1,0:T(8,128)(2,1)}, u32[]{:S(2)}) copy-start(bf16[512,512]{1,0:T(8,128)(2,1)} %constant.21.clone.odd_ref) | copy-start | bytes 1572868
  10.6 39.2 %copy-start.4 = (bf16[512,256]{1,0:T(8,128)(2,1)S(1)}, bf16[512,256]{1,0:T(8,128)(2,1)}, u32[]{:S(2)}) copy-start(bf16[512,256]{1,0:T(8,128)(2,1)} %constant.20.clone.even_ref) | copy-start | bytes 786436
  49.8 47.3 %copy-start.1 = (bf16[1536,256]{1,0:T(8,128)(2,1)S(1)}, bf16[1536,256]{1,0:T(8,128)(2,1)}, u32[]{:S(2)}) copy-start(bf16[1536,256]{1,0:T(8,128)(2,1)} %constant.22.clone.low_ref) | copy-start | bytes 2359300
  51.5 20.7 %all-to-all-start.2 = ((bf16[256,4,128]{2,1,0:T(4,128)(2,1)}), bf16[256,4,128]{2,1,0:T(4,128)(2,1)S(1)}, u32[]{:S(2)}, u32[]{:S(2)}) async-start(bf16[256,4,128]{2,1,0:T(4,128)(2,1)} %bitcast.4), calls=%async_computation.2 | async-start | bytes 524288 | tf_op jit(solution)/shard_map/all_to_all | solution.py:417

commit v4 on v3

--- a/solution.py
+++ b/solution.py
@@ -113,7 +113,8 @@
     return jnp.round(values * (LEVELS * jnp.exp2(-power))).astype(jnp.int32), power
 
 
-def arrange_kernel(initial_ref, measured_ref, pieces_ref, source, pieces, sems):
+def arrange_kernel(slab_ref, initial_ref, measured_ref, *refs):
+    far_refs, (source, pieces, sems) = refs[:SLABS], refs[SLABS:]
     loads, stores = [], []
     for chunk in range(4):
         far = (initial_ref, measured_ref)[chunk // 2].at[chunk % 2]
@@ -123,33 +124,29 @@
     heads = [jnp.zeros((16, Z), jnp.int32)] * SLABS
     for chunk in range(4):
         loads[chunk].wait()
-        for slab in range(SLABS):
+        for distance in range(SLABS):
+            slab = lax.rem(slab_ref[0] + distance, SLABS)
             for half in range(2):
                 block = 2 * chunk + half
                 codes, power = encode(source[chunk, slab + 4 * half])
                 codes = codes.astype(jnp.int16)
-                pieces[slab, pl.ds(64 * block, 32), :] = codes[:, :Z]
-                pieces[slab, pl.ds(64 * block + 32, 32), :] = codes[:, Z:]
-                heads[slab] = jnp.where(row == block, power.astype(jnp.int32), heads[slab])
-        rows = pl.ds(128 * chunk, 128)
-        if chunk == 3:
-            for slab in range(SLABS):
-                pieces[slab, pl.ds(512, 16), :] = heads[slab].astype(jnp.int16)
-            rows = pl.ds(384, 144)
-        stores.append(
-            pltpu.make_async_copy(pieces.at[:, rows], pieces_ref.at[:, rows], sems.at[4 + chunk])
-        )
+                pieces[distance, pl.ds(64 * block, 32), :] = codes[:, :Z]
+                pieces[distance, pl.ds(64 * block + 32, 32), :] = codes[:, Z:]
+                heads[distance] = jnp.where(row == block, power.astype(jnp.int32), heads[distance])
+    for distance, far in enumerate(far_refs):
+        pieces[distance, pl.ds(512, 16), :] = heads[distance].astype(jnp.int16)
+        stores.append(pltpu.make_async_copy(pieces.at[distance], far, sems.at[4 + distance]))
         stores[-1].start()
     for copy in stores:
         copy.wait()
 
 
-def arrange(initial, measured):
+def arrange(slab, initial, measured):
     return pl.pallas_call(
         arrange_kernel,
-        out_shape=jax.ShapeDtypeStruct((SLABS, 528, Z), jnp.int16),
-        in_specs=[HBM, HBM],
-        out_specs=HBM,
+        out_shape=(jax.ShapeDtypeStruct((528, Z), jnp.int16),) * SLABS,
+        in_specs=[SMEM, HBM, HBM],
+        out_specs=(HBM,) * SLABS,
         scratch_shapes=[
             pltpu.VMEM((4, 2 * SLABS, 32, R), F32),
             pltpu.VMEM((SLABS, 528, Z), jnp.int16),
@@ -158,7 +155,7 @@
         compiler_params=pltpu.CompilerParams(vmem_limit_bytes=126 << 19),
         cost_estimate=cost(1 << 20, 1 << 20),
         name="arrange",
-    )(initial, measured)
+    )(slab, initial, measured)
 
 
 def moved(values, offset, lane):
@@ -188,9 +185,13 @@
     return out
 
 
-def passes(offsets_ref, blocks_far, iterate, measured, buffers, begin):
+def slab_rows(slab, index):
+    return pl.ds(pl.multiple_of(Q * lax.rem(slab + index, SLABS), Q), Q)
+
+
+def passes(slab, offsets_ref, blocks_far, iterate, measured, buffers, begin):
     packed_ref, rows_ref, shifted, blocks, sems = buffers
-    lane = lax.broadcasted_iota(jnp.int32, (R, Z), 1)
+    lane = lax.rem(lax.broadcasted_iota(jnp.int32, (R, Z), 1) + 32 * slab, Z)
     loads = [
         pltpu.make_async_copy(blocks_far.at[half], blocks.at[half], sems.at[half]) for half in range(2)
     ]
@@ -244,7 +245,9 @@
             place_iterate(1)
     pack(0, iterate, rows_ref)
     pack(1, iterate, rows_ref)
-    packed_ref[...] = rows_ref[...].astype(packed_ref.dtype)
+    for index in range(SLABS):
+        values = rows_ref[pl.ds(Q * index, Q), :].astype(packed_ref.dtype)
+        packed_ref[slab_rows(slab, index), :] = values
 
 
 def pack(half, iterate, rows_ref):
@@ -254,31 +257,36 @@
             rows_ref[pl.ds(Q * slab + 2 * half + part, GROUPS, stride=4), :] = block
 
 
-def first_kernel(offsets_ref, pieces, blocks_far, iterate, measured, packed_ref, column, *scratch):
+def first_kernel(
+    slab_ref, offsets_ref, own, one, two, three, blocks_far, iterate, measured, packed_ref, column, *scratch
+):
+    pieces = (own, one, two, three)
     scales = []
-    for slab in range(SLABS):
-        power = pieces[slab, pl.ds(512, 16), :].astype(jnp.int32).astype(F32)
+    for piece in pieces:
+        power = piece[pl.ds(512, 16), :].astype(jnp.int32).astype(F32)
         scales.append(jnp.exp2(power) * (1.0 / LEVELS))
 
     def begin(half):
         for chunk in range(4):
             block = 2 * chunk + half
-            for slab in range(SLABS):
+            for distance, (piece, scale) in enumerate(zip(pieces, scales)):
+                rows = pl.ds(32 * ((SLABS - distance) % SLABS), 32)
                 for side in range(2):
-                    codes = pieces[slab, pl.ds(64 * block + 32 * side, 32), :].astype(jnp.int32)
-                    values = codes.astype(F32) * scales[slab][block : block + 1]
-                    column[block, pl.ds(32 * slab, 32), Z * side : Z * (side + 1)] = values
+                    codes = piece[pl.ds(64 * block + 32 * side, 32), :].astype(jnp.int32)
+                    values = codes.astype(F32) * scale[block : block + 1]
+                    column[block, rows, Z * side : Z * (side + 1)] = values
             (iterate, measured)[chunk // 2][half, chunk % 2] = column[block].T
 
-    passes(offsets_ref, blocks_far, iterate, measured, (packed_ref, *scratch), begin)
+    passes(slab_ref[0], offsets_ref, blocks_far, iterate, measured, (packed_ref, *scratch), begin)
 
 
 def second_kernel(
-    silent_ref, offsets_ref, packed_in, kept, measured, blocks_far,
+    slab_ref, silent_ref, offsets_ref, packed_in, kept, measured, blocks_far,
     packed_ref, arrived, iterate, *scratch,
 ):
     silent = silent_ref[0] != 0
-    arrived[...] = packed_in[...].astype(F32)
+    for index in range(SLABS):
+        arrived[pl.ds(Q * index, Q), :] = packed_in[slab_rows(slab_ref[0], index), :].astype(F32)
 
     def begin(half):
         for part in range(2):
@@ -292,7 +300,7 @@
                     base = jnp.where(silent, 0.0, base)
                 iterate[half, part, rows, :] = base + added
 
-    passes(offsets_ref, blocks_far, iterate, measured, (packed_ref, *scratch), begin)
+    passes(slab_ref[0], offsets_ref, blocks_far, iterate, measured, (packed_ref, *scratch), begin)
 
 
 PASS_SCRATCH = [
@@ -303,30 +311,30 @@
 ]
 
 
-def first_half(offsets, pieces, blocks):
+def first_half(slab, offsets, pieces, blocks):
     return pl.pallas_call(
         first_kernel,
         out_shape=(SPECTRUM, SPECTRUM, PACKED),
-        in_specs=[SMEM, VMEM, HBM],
+        in_specs=[SMEM, SMEM] + [VMEM] * SLABS + [HBM],
         out_specs=(VMEM,) * 3,
         scratch_shapes=[pltpu.VMEM((8, Z, R), F32)] + PASS_SCRATCH,
         compiler_params=ALONE,
         cost_estimate=cost(2 << 30, 8 << 20),
         name="first_half",
-    )(offsets, pieces, blocks)
-
-
-def later_half(silent, offsets, packed, kept, measured, blocks):
+    )(slab, offsets, *pieces, blocks)
+
+
+def later_half(slab, silent, offsets, packed, kept, measured, blocks):
     return pl.pallas_call(
         second_kernel,
         out_shape=PACKED,
-        in_specs=[SMEM, SMEM] + [VMEM] * 3 + [HBM],
+        in_specs=[SMEM] * 3 + [VMEM] * 3 + [HBM],
         out_specs=VMEM,
         scratch_shapes=[pltpu.VMEM((4 * Q, Z), F32), pltpu.VMEM((2, 2, R, Z), F32)] + PASS_SCRATCH,
         compiler_params=ALONE,
         cost_estimate=cost(2 << 30, 8 << 20),
         name="later_half",
-    )(silent, offsets, packed, kept, measured, blocks)
+    )(slab, silent, offsets, packed, kept, measured, blocks)
 
 
 def to_volume(packed_ref, tables_ref, volume):
@@ -422,11 +430,15 @@
     slab = lax.axis_index("slab").astype(jnp.int32)
     group = lax.axis_index("freq").astype(jnp.int32)
     silent = ((slab == 0) & (group == 0)).astype(jnp.int32).reshape(1)
-    pieces = lax.all_to_all(arrange(initial, measured), "slab", 0, 0, tiled=True)
-    blocks = prepare(slab.reshape(1), projector)
-    kept, measured, packed = first_half(offsets, pieces, blocks)
+    slab = slab.reshape(1)
+    pieces = list(arrange(slab, initial, measured))
+    for distance in range(1, SLABS):
+        pairs = [(i, (i + distance) % SLABS) for i in range(SLABS)]
+        pieces[distance] = lax.ppermute(pieces[distance], "slab", pairs)
+    blocks = prepare(slab, projector)
+    kept, measured, packed = first_half(slab, offsets, pieces, blocks)
     packed = exchange(middle(exchange(packed), angles, even, odd))
-    packed = later_half(silent, offsets, packed, kept, measured, blocks)
+    packed = later_half(slab, silent, offsets, packed, kept, measured, blocks)
     return last(exchange(packed), angles, angles_low)
 
 

time: 99.1 us -> 97.6 us (0.985)
  waiting for transfers between devices: 19.9 us -> 17.2 us
    ppermute x0 -> x3, starting transfers between devices: none -> 5.88 us  [on_device(): pieces[distance] = lax.ppermute(pieces[distance], 'slab', pairs)]
    all_to_all x1 -> x0, starting transfers between devices: 5.01 us -> none  [on_device(): lax.all_to_all(arrange(initial, measured), 'slab', 0, 0, tiled=True)]
    all_to_all x1 -> x0, waiting for transfers between devices: 4.51 us -> none  [on_device(): lax.all_to_all(arrange(initial, measured), 'slab', 0, 0, tiled=True)]
    ppermute x0 -> x3, waiting for transfers between devices: none -> 1.74 us  [on_device(): pieces[distance] = lax.ppermute(pieces[distance], 'slab', pairs)]
  transfers between devices with their start and end apart: 2 -> 4, of which waited for: 2 -> 2; matrix products, arithmetic and copies ran while one was open for 0% -> 0% of each run, Pallas kernels for 3% -> 3%
where the time goes in v4:
time: 97.6 us; the launch traced here: 97.4 us
  blocking collectives  50.7 us (52%)
  Pallas kernels  18.2 us (19%)
  waiting for transfers between devices  17.2 us (18%)
  starting transfers between devices  11.1 us (11%)
    all_to_all x2, blocking collectives, exchange(): lax.all_to_all(blocks, ('slab', 'freq'), 0, 0, tiled=True)  50.7 us
    all_to_all x1, waiting for transfers between devices, exchange(): lax.all_to_all(blocks, ('slab', 'freq'), 0, 0, tiled=True)  15.4 us
    ppermute x3, starting transfers between devices, on_device(): pieces[distance] = lax.ppermute(pieces[distance], 'slab', pairs)  5.88 us
    all_to_all x1, starting transfers between devices, exchange(): lax.all_to_all(blocks, ('slab', 'freq'), 0, 0, tiled=True)  5.25 us
    pallas_call x1, Pallas kernels, later_half(): pl.pallas_call(second_kernel, out_shape=PACKED, in_specs=[SMEM] * 3 + [VM...  4.66 us
    pallas_call x1, Pallas kernels, first_half(): pl.pallas_call(first_kernel, out_shape=(SPECTRUM, SPECTRUM, PACKED), in_s...  4.49 us
    pallas_call x1, Pallas kernels, prepare(): pl.pallas_call(prepare_kernel, out_shape=jax.ShapeDtypeStruct((4, 4, R, 3...  3.24 us
    pallas_call x1, Pallas kernels, arrange(): pl.pallas_call(arrange_kernel, out_shape=(jax.ShapeDtypeStruct((528, Z),...  2.42 us
  transfers between devices with their start and end apart: 4, of which 2 were waited for; matrix products, arithmetic and copies ran while one was open for 0% of the time, Pallas kernels for 3%

profile of v4, /device:TPU:1, one launch (start us, length us, event | category | flops | bytes accessed | tf_op | source)
XLA Modules:
  0.0 97.4 jit_solution(11959990715535908936)
XLA Ops:
  0.0 2.4 %arrange.1 = (s16[528,128]{1,0:T(8,128)(2,1)}, s16[528,128]{1,0:T(8,128)(2,1)}, s16[528,128]{1,0:T(8,128)(2,1)}, s16[528,128]{1,0:T(8,128)(2,1)}) custom-call(s32[1]{0:T(128)} %bitcast.slab_ref, f32[2,8,32,256]{3,2,1,0:T(8,128)} %initial_ref.1, f32[2,8,32,256]{3,2,1,0:T(8,128)} %measured_ref.1), custom_call_target="tpu_custom_call" | custom-call | flops 1048576 | bytes 1048576 | tf_op jit(solution)/shard_map/arrange/pallas_call | solution.py:145
  2.4 2.2 %collective-permute-start = (s16[528,128]{1,0:T(8,128)(2,1)}, s16[528,128]{1,0:T(8,128)(2,1)S(1)}, u32[]{:S(2)}, u32[]{:S(2)}) collective-permute-start(s16[528,128]{1,0:T(8,128)(2,1)} %get-tuple-element.13), channel_id=1, source_target_pairs={{0,64},{64,128},{128,192},{192,0},{1,65},{65,129},{129,193},{193,1... | collective-permute-start | bytes 405512 | tf_op jit(solution)/shard_map/ppermute | solution.py:437
  4.6 2.6 %collective-permute-start.1 = (s16[528,128]{1,0:T(8,128)(2,1)}, s16[528,128]{1,0:T(8,128)(2,1)S(1)}, u32[]{:S(2)}, u32[]{:S(2)}) collective-permute-start(s16[528,128]{1,0:T(8,128)(2,1)} %get-tuple-element.14), channel_id=1, source_target_pairs={{0,128},{64,192},{128,0},{192,64},{1,129},{65,193},{129,1},{193,65... | collective-permute-start | bytes 405512 | tf_op jit(solution)/shard_map/ppermute | solution.py:437
  7.2 1.1 %collective-permute-start.2 = (s16[528,128]{1,0:T(8,128)(2,1)}, s16[528,128]{1,0:T(8,128)(2,1)S(1)}, u32[]{:S(2)}, u32[]{:S(2)}) collective-permute-start(s16[528,128]{1,0:T(8,128)(2,1)} %get-tuple-element.15), channel_id=1, source_target_pairs={{0,192},{64,0},{128,64},{192,128},{1,193},{65,1},{129,65},{193,129... | collective-permute-start | bytes 405512 | tf_op jit(solution)/shard_map/ppermute | solution.py:437
  8.3 3.2 %prepare.1.blocks_far = bf16[4,4,256,768]{3,2,1,0:T(8,128)(2,1)} custom-call(s32[1]{0:T(128)} %bitcast.slab_ref, bf16[3,2,8,256,256]{4,3,2,1,0:T(8,128)(2,1)} %projector_ref.1), custom_call_target="tpu_custom_call" | custom-call | bytes 8388608 | tf_op jit(solution)/shard_map/prepare/pallas_call | solution.py:98
  11.6 0.0 copy-start
  11.6 0.0 copy-start.4
  11.6 0.0 copy-start.5
  11.6 0.0 collective-permute-done.one
  11.6 1.7 %collective-permute-done.1.two = s16[528,128]{1,0:T(8,128)(2,1)S(1)} collective-permute-done((s16[528,128]{1,0:T(8,128)(2,1)}, s16[528,128]{1,0:T(8,128)(2,1)S(1)}, u32[]{:S(2)}, u32[]{:S(2)}) %collective-permute-start.1) | collective-permute-done | bytes 135200 | tf_op jit(solution)/shard_map/ppermute | solution.py:437
  13.4 0.0 collective-permute-done.2.three
  13.4 0.0 copy-done.2
  13.4 0.0 copy-done.3
  13.4 4.5 %first_half.1 = (f32[2,2,256,128]{3,2,1,0:T(8,128)S(1)}, f32[2,2,256,128]{3,2,1,0:T(8,128)S(1)}, bf16[1024,128]{1,0:T(8,128)(2,1)S(1)}) custom-call(s32[1]{0:T(128)} %bitcast.slab_ref, s32[3]{0:T(128)S(1)} %copy-done.3, s16[528,128]{1,0:T(8,128)(2,1)S(1)} %copy-done.2, s16[528,128]{1,0:T(8,128)(2,1)S(1)} %collective-permute-done.one, ...), custom_call_target="tpu_custom_call" | custom-call | flops 2147483648 | bytes 8388608 | tf_op jit(solution)/shard_map/first_half/pallas_call | solution.py:315
  17.9 30.3 %all_to_all.15 = bf16[256,4,128]{2,1,0:T(4,128)(2,1)S(1)} all-to-all(bf16[256,4,128]{2,1,0:T(4,128)(2,1)S(1)} %bitcast.10), channel_id=1, replica_groups=mesh['slab'=4,'freq'=64] {'slab','freq'}, dimensions={0} | all-to-all | bytes 524288 | tf_op jit(solution)/shard_map/all_to_all | solution.py:425
  48.2 0.0 copy-done
  48.2 0.0 copy-done.4
  48.2 0.0 copy-start.1
  48.2 1.7 %middle.1 = bf16[1024,128]{1,0:T(8,128)(2,1)} custom-call(bf16[1024,128]{1,0:T(8,128)(2,1)S(1)} %bitcast.12, bf16[1536,256]{1,0:T(8,128)(2,1)S(1)} %copy-done, bf16[512,256]{1,0:T(8,128)(2,1)S(1)} %copy-done.5, bf16[512,512]{1,0:T(8,128)(2,1)S(1)} %copy-done.4), custom_call_target="tpu_custom_call" | custom-call | flops 1073741824 | bytes 4194304 | tf_op jit(solution)/shard_map/middle/pallas_call | solution.py:389
  49.9 5.2 %all-to-all-start.1 = ((bf16[256,4,128]{2,1,0:T(4,128)(2,1)}), bf16[256,4,128]{2,1,0:T(4,128)(2,1)S(1)}, u32[]{:S(2)}, u32[]{:S(2)}) async-start(bf16[256,4,128]{2,1,0:T(4,128)(2,1)} %bitcast.4), calls=%async_computation.1 | async-start | bytes 524288 | tf_op jit(solution)/shard_map/all_to_all | solution.py:425
  55.2 15.4 %all-to-all-done.1 = bf16[256,4,128]{2,1,0:T(4,128)(2,1)S(1)} async-done(((bf16[256,4,128]{2,1,0:T(4,128)(2,1)}), bf16[256,4,128]{2,1,0:T(4,128)(2,1)S(1)}, u32[]{:S(2)}, u32[]{:S(2)}) %all-to-all-start.1) | async-done | bytes 262176 | tf_op jit(solution)/shard_map/all_to_all | solution.py:425
  70.6 4.7 %later_half.1 = bf16[1024,128]{1,0:T(8,128)(2,1)S(1)} custom-call(s32[1]{0:T(128)} %bitcast.slab_ref, s32[1]{0:T(128)} %bitcast.1.silent_ref, s32[3]{0:T(128)S(1)} %copy-done.3, bf16[1024,128]{1,0:T(8,128)(2,1)S(1)} %bitcast.9, f32[2,2,256,128]{3,2,1,0:T(8,128)S(1)} %get-tuple-element.17.kept, f32[2,2,256,128]{3,2,1,0:T(8,128)S(1)} %get-tuple-element.18.measured, ...), custom_call_target="tpu_custom_call" | custom-call | flops 2147483648 | bytes 8388608 | tf_op jit(solution)/shard_map/later_half/pallas_call | solution.py:328
  75.3 20.4 %all_to_all.16 = bf16[256,4,128]{2,1,0:T(4,128)(2,1)S(1)} all-to-all(bf16[256,4,128]{2,1,0:T(4,128)(2,1)S(1)} %bitcast.11), channel_id=1, replica_groups=mesh['slab'=4,'freq'=64] {'slab','freq'}, dimensions={0} | all-to-all | bytes 524288 | tf_op jit(solution)/shard_map/all_to_all | solution.py:425
  95.7 1.7 %last.1 = f32[32,4,1024]{2,1,0:T(4,128)} custom-call(bf16[1024,128]{1,0:T(8,128)(2,1)S(1)} %bitcast.8, bf16[1536,256]{1,0:T(8,128)(2,1)S(1)} %copy-done, bf16[1536,256]{1,0:T(8,128)(2,1)S(1)} %copy-done.1), custom_call_target="tpu_custom_call" | custom-call | flops 536870912 | bytes 4194304 | tf_op jit(solution)/shard_map/last/pallas_call | solution.py:411
  (4 shorter events, 0.0 us)
Async XLA Ops:
  2.4 9.2 %collective-permute-start = (s16[528,128]{1,0:T(8,128)(2,1)}, s16[528,128]{1,0:T(8,128)(2,1)S(1)}, u32[]{:S(2)}, u32[]{:S(2)}) collective-permute-start(s16[528,128]{1,0:T(8,128)(2,1)} %get-tuple-element.13), channel_id=1, source_target_pairs={{0,64},{64,128},{128,192},{192,0},{1,65},{65,129},{129,193},{193,1... | collective-permute-start | bytes 405512 | tf_op jit(solution)/shard_map/ppermute | solution.py:437
  4.6 8.7 %collective-permute-start.1 = (s16[528,128]{1,0:T(8,128)(2,1)}, s16[528,128]{1,0:T(8,128)(2,1)S(1)}, u32[]{:S(2)}, u32[]{:S(2)}) collective-permute-start(s16[528,128]{1,0:T(8,128)(2,1)} %get-tuple-element.14), channel_id=1, source_target_pairs={{0,128},{64,192},{128,0},{192,64},{1,129},{65,193},{129,1},{193,65... | collective-permute-start | bytes 405512 | tf_op jit(solution)/shard_map/ppermute | solution.py:437
  7.2 6.1 %copy-start.2 = (s16[528,128]{1,0:T(8,128)(2,1)S(1)}, s16[528,128]{1,0:T(8,128)(2,1)}, u32[]{:S(2)}) copy-start(s16[528,128]{1,0:T(8,128)(2,1)} %get-tuple-element.12.own) | copy-start | bytes 405508
  7.2 6.1 %copy-start.3 = (s32[3]{0:T(128)S(1)}, s32[3]{0:T(128)}, u32[]{:S(2)}) copy-start(s32[3]{0:T(128)} %offsets_ref.3) | copy-start | bytes 40
  7.2 6.1 %collective-permute-start.2 = (s16[528,128]{1,0:T(8,128)(2,1)}, s16[528,128]{1,0:T(8,128)(2,1)S(1)}, u32[]{:S(2)}, u32[]{:S(2)}) collective-permute-start(s16[528,128]{1,0:T(8,128)(2,1)} %get-tuple-element.15), channel_id=1, source_target_pairs={{0,192},{64,0},{128,64},{192,128},{1,193},{65,1},{129,65},{193,129... | collective-permute-start | bytes 405512 | tf_op jit(solution)/shard_map/ppermute | solution.py:437
  11.6 36.6 %copy-start = (bf16[1536,256]{1,0:T(8,128)(2,1)S(1)}, bf16[1536,256]{1,0:T(8,128)(2,1)}, u32[]{:S(2)}) copy-start(bf16[1536,256]{1,0:T(8,128)(2,1)} %constant.19.clone.angles_ref.high_ref) | copy-start | bytes 2359300
  11.6 36.6 %copy-start.4 = (bf16[512,512]{1,0:T(8,128)(2,1)S(1)}, bf16[512,512]{1,0:T(8,128)(2,1)}, u32[]{:S(2)}) copy-start(bf16[512,512]{1,0:T(8,128)(2,1)} %constant.21.clone.odd_ref) | copy-start | bytes 1572868
  11.6 36.6 %copy-start.5 = (bf16[512,256]{1,0:T(8,128)(2,1)S(1)}, bf16[512,256]{1,0:T(8,128)(2,1)}, u32[]{:S(2)}) copy-start(bf16[512,256]{1,0:T(8,128)(2,1)} %constant.20.clone.even_ref) | copy-start | bytes 786436
  48.2 47.5 %copy-start.1 = (bf16[1536,256]{1,0:T(8,128)(2,1)S(1)}, bf16[1536,256]{1,0:T(8,128)(2,1)}, u32[]{:S(2)}) copy-start(bf16[1536,256]{1,0:T(8,128)(2,1)} %constant.22.clone.low_ref) | copy-start | bytes 2359300
  49.9 20.7 %all-to-all-start.1 = ((bf16[256,4,128]{2,1,0:T(4,128)(2,1)}), bf16[256,4,128]{2,1,0:T(4,128)(2,1)S(1)}, u32[]{:S(2)}, u32[]{:S(2)}) async-start(bf16[256,4,128]{2,1,0:T(4,128)(2,1)} %bitcast.4), calls=%async_computation.1 | async-start | bytes 524288 | tf_op jit(solution)/shard_map/all_to_all | solution.py:425

commit v5 on v4

--- a/solution.py
+++ b/solution.py
@@ -113,46 +113,30 @@
     return jnp.round(values * (LEVELS * jnp.exp2(-power))).astype(jnp.int32), power
 
 
-def arrange_kernel(slab_ref, initial_ref, measured_ref, *refs):
-    far_refs, (source, pieces, sems) = refs[:SLABS], refs[SLABS:]
-    loads, stores = [], []
-    for chunk in range(4):
-        far = (initial_ref, measured_ref)[chunk // 2].at[chunk % 2]
-        loads.append(pltpu.make_async_copy(far, source.at[chunk], sems.at[chunk]))
-        loads[-1].start()
+def arrange_kernel(slab_ref, initial_ref, measured_ref, *piece_refs):
     row = lax.broadcasted_iota(jnp.int32, (16, Z), 0)
-    heads = [jnp.zeros((16, Z), jnp.int32)] * SLABS
-    for chunk in range(4):
-        loads[chunk].wait()
-        for distance in range(SLABS):
-            slab = lax.rem(slab_ref[0] + distance, SLABS)
+    for distance, piece_ref in enumerate(piece_refs):
+        slab = lax.rem(slab_ref[0] + distance, SLABS)
+        head = jnp.zeros((16, Z), jnp.int32)
+        for chunk in range(4):
+            source = (initial_ref, measured_ref)[chunk // 2]
             for half in range(2):
                 block = 2 * chunk + half
-                codes, power = encode(source[chunk, slab + 4 * half])
+                codes, power = encode(source[chunk % 2, slab + 4 * half])
                 codes = codes.astype(jnp.int16)
-                pieces[distance, pl.ds(64 * block, 32), :] = codes[:, :Z]
-                pieces[distance, pl.ds(64 * block + 32, 32), :] = codes[:, Z:]
-                heads[distance] = jnp.where(row == block, power.astype(jnp.int32), heads[distance])
-    for distance, far in enumerate(far_refs):
-        pieces[distance, pl.ds(512, 16), :] = heads[distance].astype(jnp.int16)
-        stores.append(pltpu.make_async_copy(pieces.at[distance], far, sems.at[4 + distance]))
-        stores[-1].start()
-    for copy in stores:
-        copy.wait()
+                piece_ref[pl.ds(64 * block, 32), :] = codes[:, :Z]
+                piece_ref[pl.ds(64 * block + 32, 32), :] = codes[:, Z:]
+                head = jnp.where(row == block, power.astype(jnp.int32), head)
+        piece_ref[pl.ds(512, 16), :] = head.astype(jnp.int16)
 
 
 def arrange(slab, initial, measured):
     return pl.pallas_call(
         arrange_kernel,
         out_shape=(jax.ShapeDtypeStruct((528, Z), jnp.int16),) * SLABS,
-        in_specs=[SMEM, HBM, HBM],
-        out_specs=(HBM,) * SLABS,
-        scratch_shapes=[
-            pltpu.VMEM((4, 2 * SLABS, 32, R), F32),
-            pltpu.VMEM((SLABS, 528, Z), jnp.int16),
-            pltpu.SemaphoreType.DMA((8,)),
-        ],
-        compiler_params=pltpu.CompilerParams(vmem_limit_bytes=126 << 19),
+        in_specs=[SMEM, VMEM, VMEM],
+        out_specs=(VMEM,) * SLABS,
+        compiler_params=ALONE,
         cost_estimate=cost(1 << 20, 1 << 20),
         name="arrange",
     )(slab, initial, measured)
@@ -345,17 +329,29 @@
             total = total + dot(table[rows, :], block)
         return total
 
-    zero = residue(0, pl.ds(0, Q))
-    two = residue(2, pl.ds(Q, Q))
-    same, other = zero + two, zero - two
-    one = residue(1, pl.ds(2 * Q, 2 * Q))
-    three = residue(3, pl.ds(4 * Q, 2 * Q))
-    plain = one[:Q] + three[:Q]
-    turned = one[Q:] - three[Q:]
-    volume[pl.ds(8, Q), :] = same + plain
-    volume[pl.ds(8 + Q, Q), :] = other + turned
-    volume[pl.ds(8 + 2 * Q, Q), :] = same - plain
-    volume[pl.ds(8 + 3 * Q, Q), :] = other - turned
+    if len(tables_ref) == 1:
+        one, three = residue(1, pl.ds(2 * Q, Q)), residue(3, pl.ds(4 * Q, Q))
+        plain = one + three
+        zero, two = residue(0, pl.ds(0, Q)), residue(2, pl.ds(Q, Q))
+        same = zero + two
+        volume[pl.ds(8, Q), :] = same + plain
+        volume[pl.ds(8 + 2 * Q, Q), :] = same - plain
+        other = zero - two
+        turned = residue(1, pl.ds(3 * Q, Q)) - residue(3, pl.ds(5 * Q, Q))
+        volume[pl.ds(8 + Q, Q), :] = other + turned
+        volume[pl.ds(8 + 3 * Q, Q), :] = other - turned
+    else:
+        zero = residue(0, pl.ds(0, Q))
+        two = residue(2, pl.ds(Q, Q))
+        same, other = zero + two, zero - two
+        one = residue(1, pl.ds(2 * Q, 2 * Q))
+        three = residue(3, pl.ds(4 * Q, 2 * Q))
+        plain = one[:Q] + three[:Q]
+        turned = one[Q:] - three[Q:]
+        volume[pl.ds(8, Q), :] = same + plain
+        volume[pl.ds(8 + Q, Q), :] = other + turned
+        volume[pl.ds(8 + 2 * Q, Q), :] = same - plain
+        volume[pl.ds(8 + 3 * Q, Q), :] = other - turned
     volume[7:8, :] = volume[A + 7 : A + 8, :]
     volume[A + 8 : A + 9, :] = volume[8:9, :]
 

time: 97.6 us -> 97.2 us (level)
  Pallas kernels: 18.2 us -> 15.9 us
  local copies, waits for them, and re-layouts: 0.03 us -> 2.11 us
    pallas_call x1, Pallas kernels: 2.42 us -> 0.28 us  [arrange(): pl.pallas_call(arrange_kernel, out_shape=(jax.ShapeDtypeStruct((528, Z),...]
    unnamed x12 -> x14, local copies, waits for them, and re-layouts: 0.03 us -> 2.11 us
where the time goes in v5:
time: 97.2 us; the launch traced here: 96.9 us
  blocking collectives  50.7 us (52%)
  waiting for transfers between devices  17 us (17%)
  Pallas kernels  15.9 us (16%)
  starting transfers between devices  11.1 us (11%)
  local copies, waits for them, and re-layouts  2.11 us (2%)
    all_to_all x2, blocking collectives, exchange(): lax.all_to_all(blocks, ('slab', 'freq'), 0, 0, tiled=True)  50.7 us
    all_to_all x1, waiting for transfers between devices, exchange(): lax.all_to_all(blocks, ('slab', 'freq'), 0, 0, tiled=True)  15.4 us
    ppermute x3, starting transfers between devices, on_device(): pieces[distance] = lax.ppermute(pieces[distance], 'slab', pairs)  5.88 us
    all_to_all x1, starting transfers between devices, exchange(): lax.all_to_all(blocks, ('slab', 'freq'), 0, 0, tiled=True)  5.25 us
    pallas_call x1, Pallas kernels, later_half(): pl.pallas_call(second_kernel, out_shape=PACKED, in_specs=[SMEM] * 3 + [VM...  4.66 us
    pallas_call x1, Pallas kernels, first_half(): pl.pallas_call(first_kernel, out_shape=(SPECTRUM, SPECTRUM, PACKED), in_s...  4.5 us
    pallas_call x1, Pallas kernels, prepare(): pl.pallas_call(prepare_kernel, out_shape=jax.ShapeDtypeStruct((4, 4, R, 3...  3.24 us
    unnamed x14, local copies, waits for them, and re-layouts  2.11 us
  transfers between devices with their start and end apart: 4, of which 2 were waited for; matrix products, arithmetic and copies ran while one was open for 0% of the time, Pallas kernels for 3%

profile of v5, /device:TPU:1, one launch (start us, length us, event | category | flops | bytes accessed | tf_op | source)
XLA Modules:
  0.0 96.9 jit_solution(5841054896346370306)
XLA Ops:
  0.0 1.0 %copy-done.2 = f32[2,8,32,256]{3,2,1,0:T(8,128)S(1)} copy-done((f32[2,8,32,256]{3,2,1,0:T(8,128)S(1)}, f32[2,8,32,256]{3,2,1,0:T(8,128)}, u32[]{:S(2)}) %copy-start.2) | copy-done | bytes 524312
  1.0 1.0 %copy-done.3 = f32[2,8,32,256]{3,2,1,0:T(8,128)S(1)} copy-done((f32[2,8,32,256]{3,2,1,0:T(8,128)S(1)}, f32[2,8,32,256]{3,2,1,0:T(8,128)}, u32[]{:S(2)}) %copy-start.3) | copy-done | bytes 524312
  2.1 0.3 arrange.1
  2.4 2.2 %collective-permute-start = (s16[528,128]{1,0:T(8,128)(2,1)S(1)}, s16[528,128]{1,0:T(8,128)(2,1)S(1)}, u32[]{:S(2)}, u32[]{:S(2)}) collective-permute-start(s16[528,128]{1,0:T(8,128)(2,1)S(1)} %get-tuple-element.13), channel_id=1, source_target_pairs={{0,64},{64,128},{128,192},{192,0},{1,65},{65,129},{129,193},{193,1... | collective-permute-start | bytes 405512 | tf_op jit(solution)/shard_map/ppermute | solution.py:433
  4.6 2.6 %collective-permute-start.1 = (s16[528,128]{1,0:T(8,128)(2,1)S(1)}, s16[528,128]{1,0:T(8,128)(2,1)S(1)}, u32[]{:S(2)}, u32[]{:S(2)}) collective-permute-start(s16[528,128]{1,0:T(8,128)(2,1)S(1)} %get-tuple-element.14), channel_id=1, source_target_pairs={{0,128},{64,192},{128,0},{192,64},{1,129},{65,193},{129,1},{193,65... | collective-permute-start | bytes 405512 | tf_op jit(solution)/shard_map/ppermute | solution.py:433
  7.2 1.1 %collective-permute-start.2 = (s16[528,128]{1,0:T(8,128)(2,1)S(1)}, s16[528,128]{1,0:T(8,128)(2,1)S(1)}, u32[]{:S(2)}, u32[]{:S(2)}) collective-permute-start(s16[528,128]{1,0:T(8,128)(2,1)S(1)} %get-tuple-element.15), channel_id=1, source_target_pairs={{0,192},{64,0},{128,64},{192,128},{1,193},{65,1},{129,65},{193,129... | collective-permute-start | bytes 405512 | tf_op jit(solution)/shard_map/ppermute | solution.py:433
  8.3 3.2 %prepare.1.blocks_far = bf16[4,4,256,768]{3,2,1,0:T(8,128)(2,1)} custom-call(s32[1]{0:T(128)} %bitcast.slab_ref, bf16[3,2,8,256,256]{4,3,2,1,0:T(8,128)(2,1)} %projector_ref.1), custom_call_target="tpu_custom_call" | custom-call | bytes 8388608 | tf_op jit(solution)/shard_map/prepare/pallas_call | solution.py:98
  11.5 0.0 copy-start
  11.5 0.0 copy-start.5
  11.5 0.0 copy-start.6
  11.5 0.0 collective-permute-done.one
  11.6 1.5 %collective-permute-done.1.two = s16[528,128]{1,0:T(8,128)(2,1)S(1)} collective-permute-done((s16[528,128]{1,0:T(8,128)(2,1)S(1)}, s16[528,128]{1,0:T(8,128)(2,1)S(1)}, u32[]{:S(2)}, u32[]{:S(2)}) %collective-permute-start.1) | collective-permute-done | bytes 135200 | tf_op jit(solution)/shard_map/ppermute | solution.py:433
  13.1 0.0 collective-permute-done.2.three
  13.1 0.0 copy-done.4
  13.1 4.5 %first_half.1 = (f32[2,2,256,128]{3,2,1,0:T(8,128)S(1)}, f32[2,2,256,128]{3,2,1,0:T(8,128)S(1)}, bf16[1024,128]{1,0:T(8,128)(2,1)S(1)}) custom-call(s32[1]{0:T(128)} %bitcast.slab_ref, s32[3]{0:T(128)S(1)} %copy-done.4, s16[528,128]{1,0:T(8,128)(2,1)S(1)} %get-tuple-element.12.own, s16[528,128]{1,0:T(8,128)(2,1)S(1)} %collective-permute-done.one, ...), custom_call_target="tpu_custom_call" | custom-call | flops 2147483648 | bytes 8388608 | tf_op jit(solution)/shard_map/first_half/pallas_call | solution.py:299
  17.6 30.3 %all_to_all.15 = bf16[256,4,128]{2,1,0:T(4,128)(2,1)S(1)} all-to-all(bf16[256,4,128]{2,1,0:T(4,128)(2,1)S(1)} %bitcast.10), channel_id=1, replica_groups=mesh['slab'=4,'freq'=64] {'slab','freq'}, dimensions={0} | all-to-all | bytes 524288 | tf_op jit(solution)/shard_map/all_to_all | solution.py:421
  47.9 0.0 copy-done
  47.9 0.0 copy-start.1
  47.9 1.5 %middle.1 = bf16[1024,128]{1,0:T(8,128)(2,1)} custom-call(bf16[1024,128]{1,0:T(8,128)(2,1)S(1)} %bitcast.12, bf16[1536,256]{1,0:T(8,128)(2,1)S(1)} %copy-done, bf16[512,256]{1,0:T(8,128)(2,1)S(1)} %copy-done.6, bf16[512,512]{1,0:T(8,128)(2,1)S(1)} %copy-done.5), custom_call_target="tpu_custom_call" | custom-call | flops 1073741824 | bytes 4194304 | tf_op jit(solution)/shard_map/middle/pallas_call | solution.py:385
  49.4 5.2 %all-to-all-start.1 = ((bf16[256,4,128]{2,1,0:T(4,128)(2,1)}), bf16[256,4,128]{2,1,0:T(4,128)(2,1)S(1)}, u32[]{:S(2)}, u32[]{:S(2)}) async-start(bf16[256,4,128]{2,1,0:T(4,128)(2,1)} %bitcast.4), calls=%async_computation.1 | async-start | bytes 524288 | tf_op jit(solution)/shard_map/all_to_all | solution.py:421
  54.7 15.4 %all-to-all-done.1 = bf16[256,4,128]{2,1,0:T(4,128)(2,1)S(1)} async-done(((bf16[256,4,128]{2,1,0:T(4,128)(2,1)}), bf16[256,4,128]{2,1,0:T(4,128)(2,1)S(1)}, u32[]{:S(2)}, u32[]{:S(2)}) %all-to-all-start.1) | async-done | bytes 262176 | tf_op jit(solution)/shard_map/all_to_all | solution.py:421
  70.1 4.7 %later_half.1 = bf16[1024,128]{1,0:T(8,128)(2,1)S(1)} custom-call(s32[1]{0:T(128)} %bitcast.slab_ref, s32[1]{0:T(128)} %bitcast.1.silent_ref, s32[3]{0:T(128)S(1)} %copy-done.4, bf16[1024,128]{1,0:T(8,128)(2,1)S(1)} %bitcast.9, f32[2,2,256,128]{3,2,1,0:T(8,128)S(1)} %get-tuple-element.17.kept, f32[2,2,256,128]{3,2,1,0:T(8,128)S(1)} %get-tuple-element.18.measured, ...), custom_call_target="tpu_custom_call" | custom-call | flops 2147483648 | bytes 8388608 | tf_op jit(solution)/shard_map/later_half/pallas_call | solution.py:312
  74.8 20.4 %all_to_all.16 = bf16[256,4,128]{2,1,0:T(4,128)(2,1)S(1)} all-to-all(bf16[256,4,128]{2,1,0:T(4,128)(2,1)S(1)} %bitcast.11), channel_id=1, replica_groups=mesh['slab'=4,'freq'=64] {'slab','freq'}, dimensions={0} | all-to-all | bytes 524288 | tf_op jit(solution)/shard_map/all_to_all | solution.py:421
  95.2 1.7 %last.1 = f32[32,4,1024]{2,1,0:T(4,128)} custom-call(bf16[1024,128]{1,0:T(8,128)(2,1)S(1)} %bitcast.8, bf16[1536,256]{1,0:T(8,128)(2,1)S(1)} %copy-done, bf16[1536,256]{1,0:T(8,128)(2,1)S(1)} %copy-done.1), custom_call_target="tpu_custom_call" | custom-call | flops 536870912 | bytes 4194304 | tf_op jit(solution)/shard_map/last/pallas_call | solution.py:407
  (6 shorter events, 0.0 us)
Async XLA Ops:
  0.0 1.0 %copy-start.2 = (f32[2,8,32,256]{3,2,1,0:T(8,128)S(1)}, f32[2,8,32,256]{3,2,1,0:T(8,128)}, u32[]{:S(2)}) copy-start(f32[2,8,32,256]{3,2,1,0:T(8,128)} %initial_ref.1) | copy-start | bytes 1572868
  1.0 1.0 %copy-start.3 = (f32[2,8,32,256]{3,2,1,0:T(8,128)S(1)}, f32[2,8,32,256]{3,2,1,0:T(8,128)}, u32[]{:S(2)}) copy-start(f32[2,8,32,256]{3,2,1,0:T(8,128)} %measured_ref.1) | copy-start | bytes 1572868
  2.4 9.2 %collective-permute-start = (s16[528,128]{1,0:T(8,128)(2,1)S(1)}, s16[528,128]{1,0:T(8,128)(2,1)S(1)}, u32[]{:S(2)}, u32[]{:S(2)}) collective-permute-start(s16[528,128]{1,0:T(8,128)(2,1)S(1)} %get-tuple-element.13), channel_id=1, source_target_pairs={{0,64},{64,128},{128,192},{192,0},{1,65},{65,129},{129,193},{193,1... | collective-permute-start | bytes 405512 | tf_op jit(solution)/shard_map/ppermute | solution.py:433
  4.6 8.5 %collective-permute-start.1 = (s16[528,128]{1,0:T(8,128)(2,1)S(1)}, s16[528,128]{1,0:T(8,128)(2,1)S(1)}, u32[]{:S(2)}, u32[]{:S(2)}) collective-permute-start(s16[528,128]{1,0:T(8,128)(2,1)S(1)} %get-tuple-element.14), channel_id=1, source_target_pairs={{0,128},{64,192},{128,0},{192,64},{1,129},{65,193},{129,1},{193,65... | collective-permute-start | bytes 405512 | tf_op jit(solution)/shard_map/ppermute | solution.py:433
  7.2 5.9 %copy-start.4 = (s32[3]{0:T(128)S(1)}, s32[3]{0:T(128)}, u32[]{:S(2)}) copy-start(s32[3]{0:T(128)} %offsets_ref.3) | copy-start | bytes 40
  7.2 5.9 %collective-permute-start.2 = (s16[528,128]{1,0:T(8,128)(2,1)S(1)}, s16[528,128]{1,0:T(8,128)(2,1)S(1)}, u32[]{:S(2)}, u32[]{:S(2)}) collective-permute-start(s16[528,128]{1,0:T(8,128)(2,1)S(1)} %get-tuple-element.15), channel_id=1, source_target_pairs={{0,192},{64,0},{128,64},{192,128},{1,193},{65,1},{129,65},{193,129... | collective-permute-start | bytes 405512 | tf_op jit(solution)/shard_map/ppermute | solution.py:433
  11.5 36.4 %copy-start = (bf16[1536,256]{1,0:T(8,128)(2,1)S(1)}, bf16[1536,256]{1,0:T(8,128)(2,1)}, u32[]{:S(2)}) copy-start(bf16[1536,256]{1,0:T(8,128)(2,1)} %constant.19.clone.angles_ref.high_ref) | copy-start | bytes 2359300
  11.5 36.4 %copy-start.5 = (bf16[512,512]{1,0:T(8,128)(2,1)S(1)}, bf16[512,512]{1,0:T(8,128)(2,1)}, u32[]{:S(2)}) copy-start(bf16[512,512]{1,0:T(8,128)(2,1)} %constant.21.clone.odd_ref) | copy-start | bytes 1572868
  11.5 36.4 %copy-start.6 = (bf16[512,256]{1,0:T(8,128)(2,1)S(1)}, bf16[512,256]{1,0:T(8,128)(2,1)}, u32[]{:S(2)}) copy-start(bf16[512,256]{1,0:T(8,128)(2,1)} %constant.20.clone.even_ref) | copy-start | bytes 786436
  47.9 47.3 %copy-start.1 = (bf16[1536,256]{1,0:T(8,128)(2,1)S(1)}, bf16[1536,256]{1,0:T(8,128)(2,1)}, u32[]{:S(2)}) copy-start(bf16[1536,256]{1,0:T(8,128)(2,1)} %constant.22.clone.low_ref) | copy-start | bytes 2359300
  49.4 20.7 %all-to-all-start.1 = ((bf16[256,4,128]{2,1,0:T(4,128)(2,1)}), bf16[256,4,128]{2,1,0:T(4,128)(2,1)S(1)}, u32[]{:S(2)}, u32[]{:S(2)}) async-start(bf16[256,4,128]{2,1,0:T(4,128)(2,1)} %bitcast.4), calls=%async_computation.1 | async-start | bytes 524288 | tf_op jit(solution)/shard_map/all_to_all | solution.py:421

commit v6 on v5

--- a/solution.py
+++ b/solution.py
@@ -68,7 +68,7 @@
     return jnp.dot(left, right, preferred_element_type=F32)
 
 
-def prepare_kernel(slab_ref, projector_ref, blocks_ref, blocks, sems):
+def prepare_kernel(slab_ref, projector_ref, turned_ref, plain_0, plain_far, plain_ref, sems):
     slab = slab_ref[0]
     loads, stores = [], []
     for half in range(2):
@@ -76,7 +76,7 @@
             for slot in range(3):
                 copy = pltpu.make_async_copy(
                     projector_ref.at[slot, part, slab + 4 * half],
-                    blocks.at[half, 2 + part, :, pl.ds(R * slot, R)],
+                    plain_ref.at[half, part, :, pl.ds(R * slot, R)],
                     sems.at[len(loads)],
                 )
                 copy.start()
@@ -86,8 +86,10 @@
             for slot in range(3):
                 loads[6 * half + 3 * part + slot].wait()
                 cols = pl.ds(R * slot, R)
-                blocks[half, part, :, cols] = blocks[half, 2 + part, :, cols].T
-        copy = pltpu.make_async_copy(blocks.at[half], blocks_ref.at[half], sems.at[12 + half])
+                turned_ref[half, part, :, cols] = plain_ref[half, part, :, cols].T
+        if half == 0:
+            plain_0[...] = plain_ref[0]
+        copy = pltpu.make_async_copy(plain_ref.at[half], plain_far.at[half], sems.at[12 + half])
         copy.start()
         stores.append(copy)
     for copy in stores:
@@ -95,13 +97,18 @@
 
 
 def prepare(slab, projector):
+    blocks = jax.ShapeDtypeStruct((2, 2, R, 3 * R), BF16)
     return pl.pallas_call(
         prepare_kernel,
-        out_shape=jax.ShapeDtypeStruct((4, 4, R, 3 * R), BF16),
+        out_shape=(
+            blocks,
+            jax.ShapeDtypeStruct(blocks.shape[1:], BF16),
+            jax.ShapeDtypeStruct((16, 2, R, 3 * R), BF16),
+        ),
         in_specs=[SMEM, HBM],
-        out_specs=HBM,
-        scratch_shapes=[pltpu.VMEM((2, 4, R, 3 * R), BF16), pltpu.SemaphoreType.DMA((14,))],
-        compiler_params=ALONE,
+        out_specs=(VMEM, VMEM, HBM),
+        scratch_shapes=[pltpu.VMEM(blocks.shape, BF16), pltpu.SemaphoreType.DMA((14,))],
+        compiler_params=pltpu.CompilerParams(vmem_limit_bytes=100 << 19),
         cost_estimate=cost(0, 8 << 20),
         name="prepare",
     )(slab, projector)
@@ -173,15 +180,10 @@
     return pl.ds(pl.multiple_of(Q * lax.rem(slab + index, SLABS), Q), Q)
 
 
-def passes(slab, offsets_ref, blocks_far, iterate, measured, buffers, begin):
-    packed_ref, rows_ref, shifted, blocks, sems = buffers
+def passes(slab, offsets_ref, turned, plain, iterate, measured, buffers, begin, waits=None):
+    packed_ref, rows_ref, shifted = buffers
+    waits = waits or {}
     lane = lax.rem(lax.broadcasted_iota(jnp.int32, (R, Z), 1) + 32 * slab, Z)
-    loads = [
-        pltpu.make_async_copy(blocks_far.at[half], blocks.at[half], sems.at[half]) for half in range(2)
-    ]
-    for copy in loads:
-        copy.start()
-
     def place(sign, half, real, imag):
         for slot in range(3):
             rows = pl.ds(R * slot, R)
@@ -192,10 +194,8 @@
     def place_iterate(half):
         place(1, half, iterate[half, 0], iterate[half, 1])
 
-    def product(kind, half):
-        by_real = dot(blocks[half, kind], shifted[half])
-        by_imag = dot(blocks[half, kind + 1], shifted[half])
-        return by_real, by_imag
+    def product(blocks, half):
+        return [dot(blocks[half][part], shifted[half]) for part in range(2)]
 
     def place_residual(half, by_real, by_imag):
         real = measured[half, 0] - (by_real[:, :Z] - by_imag[:, Z:])
@@ -208,20 +208,22 @@
 
     begin(0)
     begin(1)
-    loads[0].wait()
     place_iterate(0)
     place_iterate(1)
-    first = product(0, 0)
-    loads[1].wait()
-    second = product(0, 1)
+    first = product(turned, 0)
+    second = product(turned, 1)
     for count in range(INNER):
         if count:
-            first = product(0, 0)
-            second = product(0, 1)
+            first = product(turned, 0)
+            second = product(turned, 1)
+        for copy in waits.pop(0, ()):
+            copy.wait()
         place_residual(0, *first)
         place_residual(1, *second)
-        first = product(2, 0)
-        second = product(2, 1)
+        first = product(plain, 0)
+        for copy in waits.pop(1, ()):
+            copy.wait()
+        second = product(plain, 1)
         update(0, *first)
         update(1, *second)
         if count + 1 < INNER:
@@ -242,8 +244,11 @@
 
 
 def first_kernel(
-    slab_ref, offsets_ref, own, one, two, three, blocks_far, iterate, measured, packed_ref, column, *scratch
+    slab_ref, offsets_ref, own, one, two, three, turned, plain_0, plain_far,
+    iterate, measured_far, packed_ref, column, measured, plain_1, sems, *scratch,
 ):
+    load = pltpu.make_async_copy(plain_far.at[1], plain_1, sems.at[1])
+    load.start()
     pieces = (own, one, two, three)
     scales = []
     for piece in pieces:
@@ -260,14 +265,28 @@
                     values = codes.astype(F32) * scale[block : block + 1]
                     column[block, rows, Z * side : Z * (side + 1)] = values
             (iterate, measured)[chunk // 2][half, chunk % 2] = column[block].T
-
-    passes(slab_ref[0], offsets_ref, blocks_far, iterate, measured, (packed_ref, *scratch), begin)
+        if half:
+            store.start()
+
+    store = pltpu.make_async_copy(measured, measured_far.at[pl.ds(0, 2)], sems.at[0])
+    turned = [turned.at[half] for half in range(2)]
+    buffers = (packed_ref, *scratch)
+    waits = {1: [load]}
+    passes(
+        slab_ref[0], offsets_ref, turned, [plain_0, plain_1], iterate, measured, buffers, begin, waits
+    )
+    store.wait()
 
 
 def second_kernel(
-    slab_ref, silent_ref, offsets_ref, packed_in, kept, measured, blocks_far,
-    packed_ref, arrived, iterate, *scratch,
+    slab_ref, silent_ref, offsets_ref, packed_in, kept, measured_far, turned, plain_far,
+    packed_ref, arrived, iterate, measured, plain, sems, *scratch,
 ):
+    loads = [pltpu.make_async_copy(measured_far.at[pl.ds(0, 2)], measured, sems.at[0])]
+    for half in range(2):
+        loads.append(pltpu.make_async_copy(plain_far.at[half], plain.at[half], sems.at[1 + half]))
+    for copy in loads:
+        copy.start()
     silent = silent_ref[0] != 0
     for index in range(SLABS):
         arrived[pl.ds(Q * index, Q), :] = packed_in[slab_rows(slab_ref[0], index), :].astype(F32)
@@ -284,41 +303,55 @@
                     base = jnp.where(silent, 0.0, base)
                 iterate[half, part, rows, :] = base + added
 
-    passes(slab_ref[0], offsets_ref, blocks_far, iterate, measured, (packed_ref, *scratch), begin)
+    buffers = (packed_ref, *scratch)
+    waits = {0: loads[:2], 1: loads[2:]}
+    turned, plain = [[blocks.at[half] for half in range(2)] for blocks in (turned, plain)]
+    passes(slab_ref[0], offsets_ref, turned, plain, iterate, measured, buffers, begin, waits)
 
 
 PASS_SCRATCH = [
     pltpu.VMEM((4 * Q, Z), F32),
     pltpu.VMEM((2, 3 * R, 2 * Z), BF16),
-    pltpu.VMEM((2, 4, R, 3 * R), BF16),
-    pltpu.SemaphoreType.DMA((2,)),
 ]
 
 
-def first_half(slab, offsets, pieces, blocks):
+def first_half(slab, offsets, pieces, turned, plain_0, plain_far):
     return pl.pallas_call(
         first_kernel,
-        out_shape=(SPECTRUM, SPECTRUM, PACKED),
-        in_specs=[SMEM, SMEM] + [VMEM] * SLABS + [HBM],
-        out_specs=(VMEM,) * 3,
-        scratch_shapes=[pltpu.VMEM((8, Z, R), F32)] + PASS_SCRATCH,
+        out_shape=(SPECTRUM, jax.ShapeDtypeStruct((48, 2, R, Z), F32), PACKED),
+        in_specs=[SMEM, SMEM] + [VMEM] * (SLABS + 2) + [HBM],
+        out_specs=(VMEM, HBM, VMEM),
+        scratch_shapes=[
+            pltpu.VMEM((8, Z, R), F32),
+            pltpu.VMEM((2, 2, R, Z), F32),
+            pltpu.VMEM((2, R, 3 * R), BF16),
+            pltpu.SemaphoreType.DMA((2,)),
+        ]
+        + PASS_SCRATCH,
         compiler_params=ALONE,
         cost_estimate=cost(2 << 30, 8 << 20),
         name="first_half",
-    )(slab, offsets, *pieces, blocks)
-
-
-def later_half(slab, silent, offsets, packed, kept, measured, blocks):
+    )(slab, offsets, *pieces, turned, plain_0, plain_far)
+
+
+def later_half(slab, silent, offsets, packed, kept, measured, turned, plain):
     return pl.pallas_call(
         second_kernel,
         out_shape=PACKED,
-        in_specs=[SMEM] * 3 + [VMEM] * 3 + [HBM],
+        in_specs=[SMEM] * 3 + [VMEM, VMEM, HBM, VMEM, HBM],
         out_specs=VMEM,
-        scratch_shapes=[pltpu.VMEM((4 * Q, Z), F32), pltpu.VMEM((2, 2, R, Z), F32)] + PASS_SCRATCH,
+        scratch_shapes=[
+            pltpu.VMEM((4 * Q, Z), F32),
+            pltpu.VMEM((2, 2, R, Z), F32),
+            pltpu.VMEM((2, 2, R, Z), F32),
+            pltpu.VMEM((2, 2, R, 3 * R), BF16),
+            pltpu.SemaphoreType.DMA((3,)),
+        ]
+        + PASS_SCRATCH,
         compiler_params=ALONE,
         cost_estimate=cost(2 << 30, 8 << 20),
         name="later_half",
-    )(slab, silent, offsets, packed, kept, measured, blocks)
+    )(slab, silent, offsets, packed, kept, measured, turned, plain)
 
 
 def to_volume(packed_ref, tables_ref, volume):
@@ -431,10 +464,10 @@
     for distance in range(1, SLABS):
         pairs = [(i, (i + distance) % SLABS) for i in range(SLABS)]
         pieces[distance] = lax.ppermute(pieces[distance], "slab", pairs)
-    blocks = prepare(slab, projector)
-    kept, measured, packed = first_half(slab, offsets, pieces, blocks)
+    turned, plain_0, plain_far = prepare(slab, projector)
+    kept, measured, packed = first_half(slab, offsets, pieces, turned, plain_0, plain_far)
     packed = exchange(middle(exchange(packed), angles, even, odd))
-    packed = later_half(slab, silent, offsets, packed, kept, measured, blocks)
+    packed = later_half(slab, silent, offsets, packed, kept, measured, turned, plain_far)
     return last(exchange(packed), angles, angles_low)
 
 

time: 97.2 us -> 97.6 us (level)
    unnamed x14 -> x16, local copies, waits for them, and re-layouts: 2.11 us -> 2.83 us
where the time goes in v6:
time: 97.6 us; the launch traced here: 97.3 us
  blocking collectives  50.7 us (52%)
  waiting for transfers between devices  17.3 us (18%)
  Pallas kernels  15.3 us (16%)
  starting transfers between devices  11.1 us (11%)
  local copies, waits for them, and re-layouts  2.83 us (3%)
    all_to_all x2, blocking collectives, exchange(): lax.all_to_all(blocks, ('slab', 'freq'), 0, 0, tiled=True)  50.7 us
    all_to_all x1, waiting for transfers between devices, exchange(): lax.all_to_all(blocks, ('slab', 'freq'), 0, 0, tiled=True)  15.4 us
    ppermute x3, starting transfers between devices, on_device(): pieces[distance] = lax.ppermute(pieces[distance], 'slab', pairs)  5.88 us
    all_to_all x1, starting transfers between devices, exchange(): lax.all_to_all(blocks, ('slab', 'freq'), 0, 0, tiled=True)  5.25 us
    pallas_call x1, Pallas kernels, first_half(): pl.pallas_call(first_kernel, out_shape=(SPECTRUM, jax.ShapeDtypeStruct((4...  4.46 us
    pallas_call x1, Pallas kernels, later_half(): pl.pallas_call(second_kernel, out_shape=PACKED, in_specs=[SMEM] * 3 + [VM...  4.38 us
    pallas_call x1, Pallas kernels, prepare(): pl.pallas_call(prepare_kernel, out_shape=(blocks, jax.ShapeDtypeStruct(bl...  2.96 us
    unnamed x16, local copies, waits for them, and re-layouts  2.83 us
  transfers between devices with their start and end apart: 4, of which 2 were waited for; matrix products, arithmetic and copies ran while one was open for 0% of the time, Pallas kernels for 3%

profile of v6, /device:TPU:1, one launch (start us, length us, event | category | flops | bytes accessed | tf_op | source)
XLA Modules:
  0.0 97.3 jit_solution(2663351082974236491)
XLA Ops:
  0.0 1.1 %copy-done.2 = f32[2,8,32,256]{3,2,1,0:T(8,128)S(1)} copy-done((f32[2,8,32,256]{3,2,1,0:T(8,128)S(1)}, f32[2,8,32,256]{3,2,1,0:T(8,128)}, u32[]{:S(2)}) %copy-start.2) | copy-done | bytes 524312
  1.1 1.0 %copy-done.3 = f32[2,8,32,256]{3,2,1,0:T(8,128)S(1)} copy-done((f32[2,8,32,256]{3,2,1,0:T(8,128)S(1)}, f32[2,8,32,256]{3,2,1,0:T(8,128)}, u32[]{:S(2)}) %copy-start.3) | copy-done | bytes 524312
  2.2 0.3 arrange.1
  2.5 2.2 %collective-permute-start = (s16[528,128]{1,0:T(8,128)(2,1)S(1)}, s16[528,128]{1,0:T(8,128)(2,1)S(1)}, u32[]{:S(2)}, u32[]{:S(2)}) collective-permute-start(s16[528,128]{1,0:T(8,128)(2,1)S(1)} %get-tuple-element.16), channel_id=1, source_target_pairs={{0,64},{64,128},{128,192},{192,0},{1,65},{65,129},{129,193},{193,1... | collective-permute-start | bytes 405512 | tf_op jit(solution)/shard_map/ppermute | solution.py:466
  4.6 2.6 %collective-permute-start.1 = (s16[528,128]{1,0:T(8,128)(2,1)S(1)}, s16[528,128]{1,0:T(8,128)(2,1)S(1)}, u32[]{:S(2)}, u32[]{:S(2)}) collective-permute-start(s16[528,128]{1,0:T(8,128)(2,1)S(1)} %get-tuple-element.17), channel_id=1, source_target_pairs={{0,128},{64,192},{128,0},{192,64},{1,129},{65,193},{129,1},{193,65... | collective-permute-start | bytes 405512 | tf_op jit(solution)/shard_map/ppermute | solution.py:466
  7.3 1.1 %collective-permute-start.2 = (s16[528,128]{1,0:T(8,128)(2,1)S(1)}, s16[528,128]{1,0:T(8,128)(2,1)S(1)}, u32[]{:S(2)}, u32[]{:S(2)}) collective-permute-start(s16[528,128]{1,0:T(8,128)(2,1)S(1)} %get-tuple-element.18), channel_id=1, source_target_pairs={{0,192},{64,0},{128,64},{192,128},{1,193},{65,1},{129,65},{193,129... | collective-permute-start | bytes 405512 | tf_op jit(solution)/shard_map/ppermute | solution.py:466
  8.3 3.0 %prepare.1 = (bf16[2,2,256,768]{3,2,1,0:T(8,128)(2,1)S(1)}, bf16[2,256,768]{2,1,0:T(8,128)(2,1)S(1)}, bf16[16,2,256,768]{3,2,1,0:T(8,128)(2,1)}) custom-call(s32[1]{0:T(128)} %bitcast.slab_ref, bf16[3,2,8,256,256]{4,3,2,1,0:T(8,128)(2,1)} %projector_ref.1), custom_call_target="tpu_custom_call" | custom-call | bytes 8388608 | tf_op jit(solution)/shard_map/prepare/pallas_call | solution.py:101
  11.3 0.0 collective-permute-done.one
  11.3 1.9 %collective-permute-done.1.two = s16[528,128]{1,0:T(8,128)(2,1)S(1)} collective-permute-done((s16[528,128]{1,0:T(8,128)(2,1)S(1)}, s16[528,128]{1,0:T(8,128)(2,1)S(1)}, u32[]{:S(2)}, u32[]{:S(2)}) %collective-permute-start.1) | collective-permute-done | bytes 135200 | tf_op jit(solution)/shard_map/ppermute | solution.py:466
  13.2 0.0 collective-permute-done.2.three
  13.2 0.7 copy-done.4
  13.8 4.5 %first_half.1 = (f32[2,2,256,128]{3,2,1,0:T(8,128)S(1)}, f32[48,2,256,128]{3,2,1,0:T(8,128)}, bf16[1024,128]{1,0:T(8,128)(2,1)S(1)}) custom-call(s32[1]{0:T(128)} %bitcast.slab_ref, s32[3]{0:T(128)S(1)} %copy-done.4, s16[528,128]{1,0:T(8,128)(2,1)S(1)} %get-tuple-element.15.own, s16[528,128]{1,0:T(8,128)(2,1)S(1)} %collective-permute-done.one, ...), custom_call_target="tpu_custom_call" | custom-call | flops 2147483648 | bytes 8388608 | tf_op jit(solution)/shard_map/first_half/pallas_call | solution.py:319
  18.3 30.3 %all_to_all.15 = bf16[256,4,128]{2,1,0:T(4,128)(2,1)S(1)} all-to-all(bf16[256,4,128]{2,1,0:T(4,128)(2,1)S(1)} %bitcast.11), channel_id=1, replica_groups=mesh['slab'=4,'freq'=64] {'slab','freq'}, dimensions={0} | all-to-all | bytes 524288 | tf_op jit(solution)/shard_map/all_to_all | solution.py:454
  48.6 0.0 copy-done
  48.6 0.0 copy-done.6
  48.6 0.0 copy-done.7
  48.6 1.5 %middle.1 = bf16[1024,128]{1,0:T(8,128)(2,1)} custom-call(bf16[1024,128]{1,0:T(8,128)(2,1)S(1)} %bitcast.12, bf16[1536,256]{1,0:T(8,128)(2,1)S(1)} %copy-done, bf16[512,256]{1,0:T(8,128)(2,1)S(1)} %copy-done.7, bf16[512,512]{1,0:T(8,128)(2,1)S(1)} %copy-done.6), custom_call_target="tpu_custom_call" | custom-call | flops 1073741824 | bytes 4194304 | tf_op jit(solution)/shard_map/middle/pallas_call | solution.py:418
  50.1 5.2 %all-to-all-start.1 = ((bf16[256,4,128]{2,1,0:T(4,128)(2,1)}), bf16[256,4,128]{2,1,0:T(4,128)(2,1)S(1)}, u32[]{:S(2)}, u32[]{:S(2)}) async-start(bf16[256,4,128]{2,1,0:T(4,128)(2,1)} %bitcast.4), calls=%async_computation.1 | async-start | bytes 524288 | tf_op jit(solution)/shard_map/all_to_all | solution.py:454
  55.4 15.4 %all-to-all-done.1 = bf16[256,4,128]{2,1,0:T(4,128)(2,1)S(1)} async-done(((bf16[256,4,128]{2,1,0:T(4,128)(2,1)}), bf16[256,4,128]{2,1,0:T(4,128)(2,1)S(1)}, u32[]{:S(2)}, u32[]{:S(2)}) %all-to-all-start.1) | async-done | bytes 262176 | tf_op jit(solution)/shard_map/all_to_all | solution.py:454
  70.8 0.0 copy-done.5
  70.8 4.4 %later_half.1 = bf16[1024,128]{1,0:T(8,128)(2,1)S(1)} custom-call(s32[1]{0:T(128)} %bitcast.slab_ref, s32[1]{0:T(128)} %bitcast.1.silent_ref, s32[3]{0:T(128)S(1)} %copy-done.5, bf16[1024,128]{1,0:T(8,128)(2,1)S(1)} %bitcast.8, f32[2,2,256,128]{3,2,1,0:T(8,128)S(1)} %get-tuple-element.23.kept, f32[48,2,256,128]{3,2,1,0:T(8,128)} %get-tuple-element.24.measured_far, ...), custom_call_target="tpu_custom_call" | custom-call | flops 2147483648 | bytes 8388608 | tf_op jit(solution)/shard_map/later_half/pallas_call | solution.py:338
  75.2 20.4 %all_to_all.16 = bf16[256,4,128]{2,1,0:T(4,128)(2,1)S(1)} all-to-all(bf16[256,4,128]{2,1,0:T(4,128)(2,1)S(1)} %bitcast.9), channel_id=1, replica_groups=mesh['slab'=4,'freq'=64] {'slab','freq'}, dimensions={0} | all-to-all | bytes 524288 | tf_op jit(solution)/shard_map/all_to_all | solution.py:454
  95.6 0.0 copy-done.1
  95.6 1.7 %last.1 = f32[32,4,1024]{2,1,0:T(4,128)} custom-call(bf16[1024,128]{1,0:T(8,128)(2,1)S(1)} %bitcast.10, bf16[1536,256]{1,0:T(8,128)(2,1)S(1)} %copy-done, bf16[1536,256]{1,0:T(8,128)(2,1)S(1)} %copy-done.1), custom_call_target="tpu_custom_call" | custom-call | flops 536870912 | bytes 4194304 | tf_op jit(solution)/shard_map/last/pallas_call | solution.py:440
  (8 shorter events, 0.0 us)
Async XLA Ops:
  0.0 48.6 %copy-start = (bf16[1536,256]{1,0:T(8,128)(2,1)S(1)}, bf16[1536,256]{1,0:T(8,128)(2,1)}, u32[]{:S(2)}) copy-start(bf16[1536,256]{1,0:T(8,128)(2,1)} %constant.19.clone.angles_ref.high_ref) | copy-start | bytes 2359300
  0.0 1.1 %copy-start.2 = (f32[2,8,32,256]{3,2,1,0:T(8,128)S(1)}, f32[2,8,32,256]{3,2,1,0:T(8,128)}, u32[]{:S(2)}) copy-start(f32[2,8,32,256]{3,2,1,0:T(8,128)} %initial_ref.1) | copy-start | bytes 1572868
  1.1 1.0 %copy-start.3 = (f32[2,8,32,256]{3,2,1,0:T(8,128)S(1)}, f32[2,8,32,256]{3,2,1,0:T(8,128)}, u32[]{:S(2)}) copy-start(f32[2,8,32,256]{3,2,1,0:T(8,128)} %measured_ref.1) | copy-start | bytes 1572868
  2.2 46.5 %copy-start.6 = (bf16[512,512]{1,0:T(8,128)(2,1)S(1)}, bf16[512,512]{1,0:T(8,128)(2,1)}, u32[]{:S(2)}) copy-start(bf16[512,512]{1,0:T(8,128)(2,1)} %constant.21.clone.odd_ref) | copy-start | bytes 1572868
  2.2 46.5 %copy-start.7 = (bf16[512,256]{1,0:T(8,128)(2,1)S(1)}, bf16[512,256]{1,0:T(8,128)(2,1)}, u32[]{:S(2)}) copy-start(bf16[512,256]{1,0:T(8,128)(2,1)} %constant.20.clone.even_ref) | copy-start | bytes 786436
  2.5 8.9 %collective-permute-start = (s16[528,128]{1,0:T(8,128)(2,1)S(1)}, s16[528,128]{1,0:T(8,128)(2,1)S(1)}, u32[]{:S(2)}, u32[]{:S(2)}) collective-permute-start(s16[528,128]{1,0:T(8,128)(2,1)S(1)} %get-tuple-element.16), channel_id=1, source_target_pairs={{0,64},{64,128},{128,192},{192,0},{1,65},{65,129},{129,193},{193,1... | collective-permute-start | bytes 405512 | tf_op jit(solution)/shard_map/ppermute | solution.py:466
  4.6 8.5 %collective-permute-start.1 = (s16[528,128]{1,0:T(8,128)(2,1)S(1)}, s16[528,128]{1,0:T(8,128)(2,1)S(1)}, u32[]{:S(2)}, u32[]{:S(2)}) collective-permute-start(s16[528,128]{1,0:T(8,128)(2,1)S(1)} %get-tuple-element.17), channel_id=1, source_target_pairs={{0,128},{64,192},{128,0},{192,64},{1,129},{65,193},{129,1},{193,65... | collective-permute-start | bytes 405512 | tf_op jit(solution)/shard_map/ppermute | solution.py:466
  7.3 63.5 %copy-start.5 = (s32[3]{0:T(128)S(1)}, s32[3]{0:T(128)}, u32[]{:S(2)}) copy-start(s32[3]{0:T(128)} %offsets_ref.3) | copy-start | bytes 40
  7.3 5.9 %collective-permute-start.2 = (s16[528,128]{1,0:T(8,128)(2,1)S(1)}, s16[528,128]{1,0:T(8,128)(2,1)S(1)}, u32[]{:S(2)}, u32[]{:S(2)}) collective-permute-start(s16[528,128]{1,0:T(8,128)(2,1)S(1)} %get-tuple-element.18), channel_id=1, source_target_pairs={{0,192},{64,0},{128,64},{192,128},{1,193},{65,1},{129,65},{193,129... | collective-permute-start | bytes 405512 | tf_op jit(solution)/shard_map/ppermute | solution.py:466
  13.2 0.7 copy-start.4
  50.1 20.7 %all-to-all-start.1 = ((bf16[256,4,128]{2,1,0:T(4,128)(2,1)}), bf16[256,4,128]{2,1,0:T(4,128)(2,1)S(1)}, u32[]{:S(2)}, u32[]{:S(2)}) async-start(bf16[256,4,128]{2,1,0:T(4,128)(2,1)} %bitcast.4), calls=%async_computation.1 | async-start | bytes 524288 | tf_op jit(solution)/shard_map/all_to_all | solution.py:454
  70.8 24.8 %copy-start.1 = (bf16[1536,256]{1,0:T(8,128)(2,1)S(1)}, bf16[1536,256]{1,0:T(8,128)(2,1)}, u32[]{:S(2)}) copy-start(bf16[1536,256]{1,0:T(8,128)(2,1)} %constant.22.clone.low_ref) | copy-start | bytes 2359300
